TPU v7x, 256 devices: a whole 4x4x8 slice. The times are simulated.
256 devices in a mesh: dp: 4 (over x_hi, core), sx: 8 (over y, x_lo), syz: 8 (over z).
Axes of the slice: x: 4 (x_hi: 2, x_lo: 2; x = x_hi * 2 + x_lo), y: 4, z: 8, core: 2. Of those that a mesh axis runs over, the one named last changes fastest.
Arguments:
- input_act: bfloat16 [4, 32, 128, 64, 128], P('dp', 'sx', 'syz'), may hold values from -6 to 6
- pre_act: bfloat16 [4, 16, 64, 64, 128], P('dp', 'sx', 'syz'), may hold values from -6 to 6
- out_grad: bfloat16 [4, 8, 32, 32, 128], P('dp', 'sx', 'syz'), may hold values from -24 to 24
- weight_one: bfloat16 [3, 3, 3, 64, 128], replicated, may hold values from -0.15625 to 0.15625
- weight_two: bfloat16 [3, 3, 3, 128, 128], replicated, may hold values from -0.109375 to 0.109375
Outputs:
- grad_input: bfloat16 [4, 32, 128, 64, 128], P('dp', 'sx', 'syz')
- grad_one: float32 [3, 3, 3, 64, 128], replicated
- grad_two: float32 [3, 3, 3, 128, 128], replicated
All inputs are finite; a program needn't handle non-finite values.
Results may differ from a plain program's by a relative error of at most 0.0049.
Values may be sent and summed in bfloat16 or wider, within the bound.
No kernel may reach another device: no remote copies, remote signals or barrier semaphores. Data moves between devices by JAX's collectives and lax.ppermute only.
A program may use at most 64 MiB of HBM per device.

v0:
```python
import jax
import jax.numpy as jnp
from jax import lax
from jax.sharding import PartitionSpec as P


def from_behind(value, axis, steps):
    count = lax.axis_size(axis)
    initial, last = (max(0, -steps), min(count, count - steps))
    return lax.ppermute(value, axis, [(source, source + steps) for source in range(initial, last)])


def lower_rims(field):
    before_x = from_behind(field[-1:], "sx", 1)
    field = jnp.concatenate([before_x, field], axis=0)
    before_y = from_behind(field[:, -1:], "syz", 1)
    return jnp.concatenate([before_y, field], axis=1)


def upper_rims(field):
    after_x = from_behind(field[:1], "sx", -1)
    field = jnp.concatenate([field, after_x], axis=0)
    after_y = from_behind(field[:, :1], "syz", -1)
    return jnp.concatenate([field, after_y], axis=1)


def filter_grad(extended, cotangent, channels):
    count_x, count_y, count_z, width_out = cotangent.shape
    padded = jnp.pad(extended, ((0, 0), (0, 0), (1, 0), (0, 0)))
    pieces = []
    for kernel_x in range(3):
        for kernel_y in range(3):
            window = lax.slice(
                padded,
                (kernel_x, kernel_y, 0, 0),
                (kernel_x + 2 * count_x - 1, kernel_y + 2 * count_y - 1, count_z + 1, 2 * channels),
                (2, 2, 1, 1),
            )
            previous = jnp.einsum(
                "xyzc,xyzo->co",
                window[:, :, :-1, channels:],
                cotangent,
                preferred_element_type=jnp.float32,
            )
            current = jnp.einsum(
                "xyzc,xyzo->co", window[:, :, 1:], cotangent, preferred_element_type=jnp.float32
            ).reshape(2, channels, width_out)
            pieces.append(jnp.concatenate([previous[None], current], axis=0))
    return jnp.stack(pieces).reshape(3, 3, 3, channels, width_out)


def data_grad(extended, weights):
    count_x = extended.shape[0] - 1
    count_y = extended.shape[1] - 1
    width_in = weights.shape[3]
    width_out = weights.shape[4]
    padded = jnp.pad(extended, ((0, 0), (0, 0), (0, 1), (0, 0)))
    paired = jnp.concatenate([padded[:, :, :-1], padded[:, :, 1:]], axis=3)
    zeroes = jnp.zeros((width_out, width_in), weights.dtype)
    kernel_taps = (((1, 0),), ((2, 0), (0, 1)))
    planes = []
    for parity_x in range(2):
        columns = []
        for parity_y in range(2):
            summed = None
            for kernel_x, offset_x in kernel_taps[parity_x]:
                for kernel_y, offset_y in kernel_taps[parity_y]:
                    stencil = weights[kernel_x, kernel_y]
                    matrix = jnp.concatenate(
                        [
                            jnp.concatenate([stencil[1].T, stencil[2].T], axis=1),
                            jnp.concatenate([zeroes, stencil[0].T], axis=1),
                        ],
                        axis=0,
                    )
                    window = paired[offset_x : offset_x + count_x, offset_y : offset_y + count_y]
                    product = jnp.einsum(
                        "xyzk,kc->xyzc", window, matrix, preferred_element_type=jnp.float32
                    )
                    summed = product if summed is None else summed + product
            columns.append(summed)
        stacked = jnp.stack(columns, axis=2)
        planes.append(stacked.reshape(count_x, 2 * count_y, stacked.shape[3], stacked.shape[4]))
    assembled = jnp.stack(planes, axis=1)
    return assembled.reshape(2 * count_x, 2 * count_y, assembled.shape[3], assembled.shape[4])


def on_device(input_act, pre_act, out_grad, weight_one, weight_two):
    source = input_act[0]
    saved = pre_act[0]
    incoming = out_grad[0]
    channels_in = weight_one.shape[3]
    channels_mid = weight_one.shape[4]
    mid_x, mid_y, mid_z = (saved.shape[0], saved.shape[1], saved.shape[2])
    pre_float = saved.astype(jnp.float32)
    activation = jnp.where(pre_float > 0, pre_float, 0.3 * pre_float).astype(jnp.bfloat16)
    act_pairs = activation.reshape(mid_x, mid_y, mid_z // 2, 2 * channels_mid)
    grad_act = data_grad(upper_rims(incoming), weight_two).reshape(
        mid_x, mid_y, mid_z, channels_mid
    )
    grad_pre = (grad_act * jnp.where(pre_float > 0, 1.0, 0.3)).astype(jnp.bfloat16)
    grad_two = filter_grad(lower_rims(act_pairs), incoming, channels_mid)
    grad_one = filter_grad(lower_rims(source), grad_pre, channels_in)
    grad_input = data_grad(upper_rims(grad_pre), weight_one).astype(jnp.bfloat16)[None]
    devices_all = lax.axis_size("dp") * lax.axis_size("sx") * lax.axis_size("syz")
    cells_two = incoming.shape[0] * incoming.shape[1] * incoming.shape[2]
    grad_one = grad_one * float(devices_all * mid_x * mid_y * mid_z) ** (-0.5)
    grad_two = grad_two * float(devices_all * cells_two) ** (-0.5)
    grad_one, grad_two = lax.psum((grad_one, grad_two), ("dp", "sx", "syz"))
    return (grad_input, grad_one, grad_two)


def solution(mesh):
    in_specs = (
        P("dp", "sx", "syz", None, None),
        P("dp", "sx", "syz", None, None),
        P("dp", "sx", "syz", None, None),
        P(),
        P(),
    )
    out_specs = (P("dp", "sx", "syz", None, None), P(), P())
    return jax.shard_map(
        on_device, mesh=mesh, in_specs=in_specs, out_specs=out_specs, check_vma=False
    )
```

profile of v0, /device:TPU:1, one launch (start us, length us, event | category | flops | bytes accessed | tf_op | source)
XLA Modules:
  0.0 409.8 jit_solution(12811735037101333327)
XLA Ops:
  7.2 1.4 collective-permute-start
  8.7 2.0 copy.221
  11.5 5.4 %collective-permute-start.4 = (bf16[1,16,64,128]{2,3,1,0:T(8,128)(2,1)}, bf16[1,16,64,128]{2,3,1,0:T(8,128)(2,1)}, u32[]{:S(2)}, u32[]{:S(2)}) collective-permute-start(bf16[1,16,64,128]{2,3,1,0:T(8,128)(2,1)} %slice_bitcast_fusion), channel_id=1, source_target_pairs={{0,8},{8,16},{16,24},{24,32},{32,40},{40,48},{48,56},{1,9},{9,17},... | collective-permute-start | bytes 786440 | tf_op jit(solution)/shard_map/ppermute | solution.py:10
  17.8 1.7 fusion.346
  21.2 1.3 collective-permute-start.1
  22.5 1.5 fusion.347
  24.0 1.4 copy.324
  25.4 1.4 copy.323
  26.8 1.4 copy.322
  28.2 1.5 copy.288
  29.7 1.5 copy.287
  31.2 1.5 copy.286
  32.7 1.5 copy.291
  34.1 1.5 copy.290
  35.6 1.5 copy.289
  37.1 1.5 copy.294
  38.5 1.5 copy.293
  40.0 1.5 copy.292
  42.2 1.5 copy.296
  79.1 1.3 collective-permute-start.2
  82.1 4.1 %collective-permute-start.6 = (bf16[1,8,32,256]{3,2,1,0:T(8,128)(2,1)S(1)}, bf16[1,8,32,256]{3,2,1,0:T(8,128)(2,1)S(1)}, u32[]{:S(2)}, u32[]{:S(2)}) collective-permute-start(bf16[1,8,32,256]{3,2,1,0:T(8,128)(2,1)S(1)} %slice.626), channel_id=1, source_target_pairs={{0,8},{8,16},{16,24},{24,32},{32,40},{40,48},{48,56},{1,9},{9,17},... | collective-permute-start | bytes 393224 | tf_op jit(solution)/shard_map/ppermute | solution.py:10
  88.1 4.3 %collective-permute-start.7 = (bf16[3,1,32,256]{3,2,1,0:T(8,128)(2,1)S(1)}, bf16[3,1,32,256]{3,2,1,0:T(8,128)(2,1)S(1)}, u32[]{:S(2)}, u32[]{:S(2)}) collective-permute-start(bf16[3,1,32,256]{3,2,1,0:T(8,128)(2,1)S(1)} %pad_maximum_fusion.8), channel_id=1, source_target_pairs={{0,1},{1,2},{2,3},{3,4},{4,5},{5,6},{6,7},{8,9},{9,10},{10,11},{11... | collective-permute-start | bytes 147464 | tf_op jit(solution)/shard_map/ppermute | solution.py:10
  93.1 1.3 collective-permute-start.3
  99.8 2.1 fusion.187
  101.8 2.1 fusion.183
  103.9 1.4 broadcast_multiply_fusion
  106.2 4.4 %collective-permute-start.5 = (bf16[5,1,64,128]{2,3,1,0:T(8,128)(2,1)S(1)}, bf16[5,1,64,128]{2,3,1,0:T(8,128)(2,1)S(1)}, u32[]{:S(2)}, u32[]{:S(2)}) collective-permute-start(bf16[5,1,64,128]{2,3,1,0:T(8,128)(2,1)S(1)} %pad_maximum_fusion.6), channel_id=1, source_target_pairs={{0,1},{1,2},{2,3},{3,4},{4,5},{5,6},{6,7},{8,9},{9,10},{10,11},{11... | collective-permute-start | bytes 245768 | tf_op jit(solution)/shard_map/ppermute | solution.py:10
  110.6 2.1 fusion.179
  112.7 2.6 fusion.3
  126.4 1.4 fusion.12
  135.0 264.4 %all-reduce.25.cloned.1.call-done = (f32[3,3,3,64,128]{4,3,2,1,0:T(8,128)}, f32[3,3,3,128,128]{4,3,2,1,0:T(8,128)}) async-done(((f32[3,3,3,64,128]{4,3,2,1,0:T(8,128)}, f32[3,3,3,128,128]{4,3,2,1,0:T(8,128)}), (f32[3,3,3,64,128]{4,3,2,1,0:T(8,128)}, f32[3,3,3,128,128]{4,3,2,1,0:T(8,128)})) %all-reduce.25.cloned.1.call-update) | async-done | bytes 2654224 | tf_op jit(solution)/shard_map/psum | solution.py:109
  399.4 2.3 copy.388
  (331 shorter events, 68.1 us)
Async XLA Ops:
  7.2 392.2 %all-reduce.25.cloned.1.call-start = ((), (), s32[]{:S(2)}) async-start(), calls=%async_computation | async-start | bytes 5308416 | tf_op jit(solution)/shard_map/psum | solution.py:109
  7.2 13.3 %collective-permute-start = (bf16[1,4,32,128]{3,2,1,0:T(8,128)(2,1)}, bf16[1,4,32,128]{3,2,1,0:T(8,128)(2,1)S(1)}, u32[]{:S(2)}, u32[]{:S(2)}) collective-permute-start(bf16[1,4,32,128]{3,2,1,0:T(8,128)(2,1)} %bitcast.710), channel_id=1, source_target_pairs={{8,0},{16,8},{24,16},{32,24},{40,32},{48,40},{56,48},{9,1},{17,9},... | collective-permute-start | bytes 98312 | tf_op jit(solution)/shard_map/ppermute | solution.py:10
  11.5 93.8 %collective-permute-start.4 = (bf16[1,16,64,128]{2,3,1,0:T(8,128)(2,1)}, bf16[1,16,64,128]{2,3,1,0:T(8,128)(2,1)}, u32[]{:S(2)}, u32[]{:S(2)}) collective-permute-start(bf16[1,16,64,128]{2,3,1,0:T(8,128)(2,1)} %slice_bitcast_fusion), channel_id=1, source_target_pairs={{0,8},{8,16},{16,24},{24,32},{32,40},{40,48},{48,56},{1,9},{9,17},... | collective-permute-start | bytes 786440 | tf_op jit(solution)/shard_map/ppermute | solution.py:10
  20.3 23.4 %copy-start.7 = (bf16[1,1,1,128,128]{4,3,2,1,0:T(8,128)(2,1)S(1)}, bf16[1,1,1,128,128]{4,3,2,1,0:T(8,128)(2,1)}, u32[]{:S(2)}) copy-start(bf16[1,1,1,128,128]{4,3,2,1,0:T(8,128)(2,1)} %get-tuple-element.18) | copy-start | bytes 98308
  20.3 24.1 %copy-start.6 = (bf16[1,1,1,128,128]{4,3,2,1,0:T(8,128)(2,1)S(1)}, bf16[1,1,1,128,128]{4,3,2,1,0:T(8,128)(2,1)}, u32[]{:S(2)}) copy-start(bf16[1,1,1,128,128]{4,3,2,1,0:T(8,128)(2,1)} %get-tuple-element.31) | copy-start | bytes 98308
  20.4 24.8 %copy-start.5 = (bf16[1,1,1,128,128]{4,3,2,1,0:T(8,128)(2,1)S(1)}, bf16[1,1,1,128,128]{4,3,2,1,0:T(8,128)(2,1)}, u32[]{:S(2)}) copy-start(bf16[1,1,1,128,128]{4,3,2,1,0:T(8,128)(2,1)} %get-tuple-element.32) | copy-start | bytes 98308
  20.4 34.9 %copy-start.23 = (bf16[1,1,1,64,128]{4,3,2,1,0:T(8,128)(2,1)S(1)}, bf16[1,1,1,64,128]{4,3,2,1,0:T(8,128)(2,1)}, u32[]{:S(2)}) copy-start(bf16[1,1,1,64,128]{4,3,2,1,0:T(8,128)(2,1)} %get-tuple-element.55) | copy-start | bytes 49156
  20.4 35.6 %copy-start.22 = (bf16[1,1,1,64,128]{4,3,2,1,0:T(8,128)(2,1)S(1)}, bf16[1,1,1,64,128]{4,3,2,1,0:T(8,128)(2,1)}, u32[]{:S(2)}) copy-start(bf16[1,1,1,64,128]{4,3,2,1,0:T(8,128)(2,1)} %get-tuple-element.56) | copy-start | bytes 49156
  20.4 36.3 %copy-start.21 = (bf16[1,1,1,64,128]{4,3,2,1,0:T(8,128)(2,1)S(1)}, bf16[1,1,1,64,128]{4,3,2,1,0:T(8,128)(2,1)}, u32[]{:S(2)}) copy-start(bf16[1,1,1,64,128]{4,3,2,1,0:T(8,128)(2,1)} %get-tuple-element.57) | copy-start | bytes 49156
  20.4 37.0 %copy-start.20 = (bf16[1,1,1,64,128]{4,3,2,1,0:T(8,128)(2,1)S(1)}, bf16[1,1,1,64,128]{4,3,2,1,0:T(8,128)(2,1)}, u32[]{:S(2)}) copy-start(bf16[1,1,1,64,128]{4,3,2,1,0:T(8,128)(2,1)} %get-tuple-element.58) | copy-start | bytes 49156
  20.4 37.7 %copy-start.19 = (bf16[1,1,1,64,128]{4,3,2,1,0:T(8,128)(2,1)S(1)}, bf16[1,1,1,64,128]{4,3,2,1,0:T(8,128)(2,1)}, u32[]{:S(2)}) copy-start(bf16[1,1,1,64,128]{4,3,2,1,0:T(8,128)(2,1)} %get-tuple-element.59) | copy-start | bytes 49156
  20.4 38.4 %copy-start.18 = (bf16[1,1,1,64,128]{4,3,2,1,0:T(8,128)(2,1)S(1)}, bf16[1,1,1,64,128]{4,3,2,1,0:T(8,128)(2,1)}, u32[]{:S(2)}) copy-start(bf16[1,1,1,64,128]{4,3,2,1,0:T(8,128)(2,1)} %get-tuple-element.60) | copy-start | bytes 49156
  20.4 39.1 %copy-start.17 = (bf16[1,1,1,64,128]{4,3,2,1,0:T(8,128)(2,1)S(1)}, bf16[1,1,1,64,128]{4,3,2,1,0:T(8,128)(2,1)}, u32[]{:S(2)}) copy-start(bf16[1,1,1,64,128]{4,3,2,1,0:T(8,128)(2,1)} %get-tuple-element.61) | copy-start | bytes 49156
  20.4 39.2 %copy-start.16 = (bf16[1,1,1,64,128]{4,3,2,1,0:T(8,128)(2,1)S(1)}, bf16[1,1,1,64,128]{4,3,2,1,0:T(8,128)(2,1)}, u32[]{:S(2)}) copy-start(bf16[1,1,1,64,128]{4,3,2,1,0:T(8,128)(2,1)} %get-tuple-element.62) | copy-start | bytes 49156
  20.4 39.4 %copy-start.15 = (bf16[1,1,1,64,128]{4,3,2,1,0:T(8,128)(2,1)S(1)}, bf16[1,1,1,64,128]{4,3,2,1,0:T(8,128)(2,1)}, u32[]{:S(2)}) copy-start(bf16[1,1,1,64,128]{4,3,2,1,0:T(8,128)(2,1)} %get-tuple-element.63) | copy-start | bytes 49156
  20.5 39.5 %copy-start.14 = (bf16[1,1,1,64,128]{4,3,2,1,0:T(8,128)(2,1)S(1)}, bf16[1,1,1,64,128]{4,3,2,1,0:T(8,128)(2,1)}, u32[]{:S(2)}) copy-start(bf16[1,1,1,64,128]{4,3,2,1,0:T(8,128)(2,1)} %get-tuple-element.64) | copy-start | bytes 49156
  20.5 40.2 %copy-start.13 = (bf16[1,1,1,64,128]{4,3,2,1,0:T(8,128)(2,1)S(1)}, bf16[1,1,1,64,128]{4,3,2,1,0:T(8,128)(2,1)}, u32[]{:S(2)}) copy-start(bf16[1,1,1,64,128]{4,3,2,1,0:T(8,128)(2,1)} %get-tuple-element.65) | copy-start | bytes 49156
  20.5 40.9 %copy-start.12 = (bf16[1,1,1,64,128]{4,3,2,1,0:T(8,128)(2,1)S(1)}, bf16[1,1,1,64,128]{4,3,2,1,0:T(8,128)(2,1)}, u32[]{:S(2)}) copy-start(bf16[1,1,1,64,128]{4,3,2,1,0:T(8,128)(2,1)} %get-tuple-element.66) | copy-start | bytes 49156
  20.5 41.7 %copy-start.11 = (bf16[1,1,1,64,128]{4,3,2,1,0:T(8,128)(2,1)S(1)}, bf16[1,1,1,64,128]{4,3,2,1,0:T(8,128)(2,1)}, u32[]{:S(2)}) copy-start(bf16[1,1,1,64,128]{4,3,2,1,0:T(8,128)(2,1)} %get-tuple-element.67) | copy-start | bytes 49156
  20.5 42.4 %copy-start.10 = (bf16[1,1,1,64,128]{4,3,2,1,0:T(8,128)(2,1)S(1)}, bf16[1,1,1,64,128]{4,3,2,1,0:T(8,128)(2,1)}, u32[]{:S(2)}) copy-start(bf16[1,1,1,64,128]{4,3,2,1,0:T(8,128)(2,1)} %get-tuple-element.68) | copy-start | bytes 49156
  20.5 43.1 %copy-start.9 = (bf16[1,1,1,64,128]{4,3,2,1,0:T(8,128)(2,1)S(1)}, bf16[1,1,1,64,128]{4,3,2,1,0:T(8,128)(2,1)}, u32[]{:S(2)}) copy-start(bf16[1,1,1,64,128]{4,3,2,1,0:T(8,128)(2,1)} %get-tuple-element.69) | copy-start | bytes 49156
  20.5 43.8 %copy-start.8 = (bf16[1,1,1,64,128]{4,3,2,1,0:T(8,128)(2,1)S(1)}, bf16[1,1,1,64,128]{4,3,2,1,0:T(8,128)(2,1)}, u32[]{:S(2)}) copy-start(bf16[1,1,1,64,128]{4,3,2,1,0:T(8,128)(2,1)} %get-tuple-element.70) | copy-start | bytes 49156
  21.2 49.7 %collective-permute-start.1 = (bf16[2,1,32,128]{3,2,1,0:T(8,128)(2,1)}, bf16[2,1,32,128]{3,2,1,0:T(8,128)(2,1)S(1)}, u32[]{:S(2)}, u32[]{:S(2)}) collective-permute-start(bf16[2,1,32,128]{3,2,1,0:T(8,128)(2,1)} %pad_maximum_fusion.10), channel_id=1, source_target_pairs={{1,0},{2,1},{3,2},{4,3},{5,4},{6,5},{7,6},{9,8},{10,9},{11,10},{12... | collective-permute-start | bytes 49160 | tf_op jit(solution)/shard_map/ppermute | solution.py:10
  42.2 25.8 %copy-start.25 = (bf16[1,1,1,64,128]{4,3,2,1,0:T(8,128)(2,1)S(1)}, bf16[1,1,1,64,128]{4,3,2,1,0:T(8,128)(2,1)}, u32[]{:S(2)}) copy-start(bf16[1,1,1,64,128]{4,3,2,1,0:T(8,128)(2,1)} %get-tuple-element.76) | copy-start | bytes 49156
  42.2 26.5 %copy-start.24 = (bf16[1,1,1,64,128]{4,3,2,1,0:T(8,128)(2,1)S(1)}, bf16[1,1,1,64,128]{4,3,2,1,0:T(8,128)(2,1)}, u32[]{:S(2)}) copy-start(bf16[1,1,1,64,128]{4,3,2,1,0:T(8,128)(2,1)} %get-tuple-element.77) | copy-start | bytes 49156
  44.4 22.8 %copy-start.26 = (bf16[1,1,1,64,128]{4,3,2,1,0:T(8,128)(2,1)S(1)}, bf16[1,1,1,64,128]{4,3,2,1,0:T(8,128)(2,1)}, u32[]{:S(2)}) copy-start(bf16[1,1,1,64,128]{4,3,2,1,0:T(8,128)(2,1)} %get-tuple-element.75) | copy-start | bytes 49156
  48.8 23.3 %copy-start.54 = (bf16[1,1,1,128,128]{3,4,2,1,0:T(8,128)(2,1)S(1)}, bf16[1,1,1,128,128]{3,4,2,1,0:T(8,128)(2,1)}, u32[]{:S(2)}) copy-start(bf16[1,1,1,128,128]{3,4,2,1,0:T(8,128)(2,1)} %copy.291) | copy-start | bytes 98308
  79.1 13.3 %collective-permute-start.2 = (bf16[1,8,64,128]{3,2,1,0:T(8,128)(2,1)}, bf16[1,8,64,128]{3,2,1,0:T(8,128)(2,1)}, u32[]{:S(2)}, u32[]{:S(2)}) collective-permute-start(bf16[1,8,64,128]{3,2,1,0:T(8,128)(2,1)} %slice.659), channel_id=1, source_target_pairs={{8,0},{16,8},{24,16},{32,24},{40,32},{48,40},{56,48},{9,1},{17,9},... | collective-permute-start | bytes 393224 | tf_op jit(solution)/shard_map/ppermute | solution.py:10
  82.1 6.0 %collective-permute-start.6 = (bf16[1,8,32,256]{3,2,1,0:T(8,128)(2,1)S(1)}, bf16[1,8,32,256]{3,2,1,0:T(8,128)(2,1)S(1)}, u32[]{:S(2)}, u32[]{:S(2)}) collective-permute-start(bf16[1,8,32,256]{3,2,1,0:T(8,128)(2,1)S(1)} %slice.626), channel_id=1, source_target_pairs={{0,8},{8,16},{16,24},{24,32},{32,40},{40,48},{48,56},{1,9},{9,17},... | collective-permute-start | bytes 393224 | tf_op jit(solution)/shard_map/ppermute | solution.py:10
  88.1 6.3 %collective-permute-start.7 = (bf16[3,1,32,256]{3,2,1,0:T(8,128)(2,1)S(1)}, bf16[3,1,32,256]{3,2,1,0:T(8,128)(2,1)S(1)}, u32[]{:S(2)}, u32[]{:S(2)}) collective-permute-start(bf16[3,1,32,256]{3,2,1,0:T(8,128)(2,1)S(1)} %pad_maximum_fusion.8), channel_id=1, source_target_pairs={{0,1},{1,2},{2,3},{3,4},{4,5},{5,6},{6,7},{8,9},{9,10},{10,11},{11... | collective-permute-start | bytes 147464 | tf_op jit(solution)/shard_map/ppermute | solution.py:10
  93.1 5.5 %collective-permute-start.3 = (bf16[3,1,64,128]{3,2,1,0:T(8,128)(2,1)S(1)}, bf16[3,1,64,128]{3,2,1,0:T(8,128)(2,1)S(1)}, u32[]{:S(2)}, u32[]{:S(2)}) collective-permute-start(bf16[3,1,64,128]{3,2,1,0:T(8,128)(2,1)S(1)} %pad_maximum_fusion.9), channel_id=1, source_target_pairs={{1,0},{2,1},{3,2},{4,3},{5,4},{6,5},{7,6},{9,8},{10,9},{11,10},{12... | collective-permute-start | bytes 147464 | tf_op jit(solution)/shard_map/ppermute | solution.py:10
  106.2 6.5 %collective-permute-start.5 = (bf16[5,1,64,128]{2,3,1,0:T(8,128)(2,1)S(1)}, bf16[5,1,64,128]{2,3,1,0:T(8,128)(2,1)S(1)}, u32[]{:S(2)}, u32[]{:S(2)}) collective-permute-start(bf16[5,1,64,128]{2,3,1,0:T(8,128)(2,1)S(1)} %pad_maximum_fusion.6), channel_id=1, source_target_pairs={{0,1},{1,2},{2,3},{3,4},{4,5},{5,6},{6,7},{8,9},{9,10},{10,11},{11... | collective-permute-start | bytes 245768 | tf_op jit(solution)/shard_map/ppermute | solution.py:10
  (58 other events, 319.0 us)
Sparse Core Ops, SparseCore 0:
  124.4 274.9 all-reduce.24
where the time goes:
time: 413 us; the launch traced here: 410 us
  waiting for transfers between devices  265 us (64%)
  local copies, waits for them, and re-layouts  67.6 us (16%)
  matrix products  24.9 us (6%)
  starting transfers between devices  23.4 us (6%)
  between operations  15.7 us (4%)
  other arithmetic  13 us (3%)
    psum x1, waiting for transfers between devices, on_device(): grad_one, grad_two = lax.psum((grad_one, grad_two), ('dp', 'sx', 'syz'))  264 us
    unnamed x223, local copies, waits for them, and re-layouts  54.1 us
    ppermute x8, starting transfers between devices, from_behind(): lax.ppermute(value, axis, [(source, source + steps) for source in range(i...  23.4 us
    dot_general x18, matrix products, data_grad(): jnp.einsum('xyzk,kc->xyzc', window, matrix, preferred_element_type=jnp.fl...  16.9 us
  transfers between devices with their start and end apart: 9, of which 2 were waited for; matrix products, arithmetic and copies ran while one was open for 21% of the time, Pallas kernels for 0%

commit v1 on v0

v1 whole, which is shorter than its diff:
```python
import functools

import jax
import jax.numpy as jnp
from jax import lax
from jax.experimental import pallas as pl
from jax.experimental.pallas import tpu as pltpu
from jax.sharding import Mesh
from jax.sharding import PartitionSpec as P

BF = jnp.bfloat16
F32 = jnp.float32

CX, CY, CZ = 1, 4, 32
MX, MY, MZ = 2, 8, 64
CIN, C1, C2 = 64, 128, 128
EX, EY = MX + 1, MY + 1
CHUNK = 88
GROUP = 32
HALF = CHUNK * GROUP
ROWS_ONE = 27 * CIN
ROWS_TWO = 27 * C1
ROWS = 2 * HALF
SCALE_ONE = float(4 * 16 * 64 * 64) ** (-0.5)
SCALE_TWO = float(4 * 8 * 32 * 32) ** (-0.5)

TAP = ((1, 1), (0, 0), (1, 0))
TAPS = (((1, 0),), ((2, 0), (0, 1)))
SLOT = (2, 0, 1)


def nt(a, b):
    return lax.dot_general(a, b, (((1,), (1,)), ((), ())), preferred_element_type=F32)


def nn(a, b):
    return lax.dot_general(a, b, (((1,), (0,)), ((), ())), preferred_element_type=F32)


def next_row(value, period):
    rows = value.shape[0]
    rolled = pltpu.roll(value, rows - 1, 0)
    row = lax.broadcasted_iota(jnp.int32, value.shape, 0)
    return jnp.where(row % period == period - 1, 0.0, rolled)


def main_kernel(
    core_ref, u_ref, pre_ref, og_ref, hx_ref, hy_ref, hc_ref, w1_ref, w2_ref,
    a_ref, keep_ref, send_ref,
    b_s, r2_s, ga_s, act_s, u2t_s, u1t_s, buf_s,
):
    zero = jnp.zeros((C1, C2), BF)
    for kx in range(3):
        for ky in range(3):
            t = kx * 3 + ky
            r2_s[t, 0:C1, 0:C2] = w2_ref[kx, ky, 1]
            r2_s[t, 0:C1, C2:] = zero
            r2_s[t, C1:, 0:C2] = w2_ref[kx, ky, 2]
            r2_s[t, C1:, C2:] = w2_ref[kx, ky, 0]

    def put_b(at, value):
        n = value.shape[0]
        b_s[at : at + n, 0:C2] = value
        b_s[at : at + n, C2:] = next_row(value.astype(F32), CZ).astype(BF)

    put_b(0, og_ref[0, 0].reshape(CY * CZ, C2))
    put_b(CY * CZ, hy_ref[0:CZ])
    put_b((CY + 1) * CZ, hx_ref[0 : CY * CZ])
    put_b((2 * CY + 1) * CZ, hc_ref[0:CZ])

    def put_ga(mx, my, value):
        base = (mx * EY + my) * MZ
        ga_s[pl.ds(base, CZ, stride=2), :] = value[:, 0:C1]
        ga_s[pl.ds(base + 1, CZ, stride=2), :] = value[:, C1:]

    def b_rows(i, j, n):
        at = (i * (CY + 1) + j) * CZ
        return b_s[at : at + n * CZ, :]

    for px in range(2):
        for i in range(2 - px):
            for py in range(2):
                n = CY + 1 - py
                total = None
                for kx, dx in TAPS[px]:
                    for ky, dy in TAPS[py]:
                        part = nt(b_rows(i + dx, dy, n), r2_s[kx * 3 + ky])
                        total = part if total is None else total + part
                for j in range(n):
                    put_ga(2 * i + px, 2 * j + py, total[j * CZ : (j + 1) * CZ])

    def put_a(at, pre):
        n = pre.shape[0]
        slope = jnp.where(pre.astype(F32) > 0, 1.0, 0.3)
        value = ga_s[at : at + n, :] * slope
        a_ref[at : at + n, 0:C1] = value.astype(BF)
        a_ref[at : at + n, C1:] = next_row(value, MZ).astype(BF)

    own = MY * MZ
    for mx in range(MX):
        put_a(mx * EY * MZ, pre_ref[0, mx].reshape(own, C1))
        put_a((mx * EY + MY) * MZ, hy_ref[CZ + mx * MZ : CZ + (mx + 1) * MZ])
    put_a(MX * EY * MZ, hx_ref[CY * CZ : CY * CZ + own])
    put_a((MX * EY + MY) * MZ, hc_ref[CZ : CZ + MZ])

    for mx in range(MX):
        pre = pre_ref[0, mx].reshape(own, C1).astype(F32)
        act_s[mx * own : (mx + 1) * own, :] = jnp.where(pre > 0, pre, 0.3 * pre)
    for px in range(2):
        for py in range(2):
            for s in range(2):
                rows = [
                    act_s[pl.ds((px * MY + 2 * j + py) * MZ + s, CZ, stride=2), :]
                    for j in range(CY)
                ]
                u2t_s[px * 2 + py, s * C1 : (s + 1) * C1, :] = jnp.concatenate(rows, 0).T.astype(BF)

    buf_s[ROWS_ONE + ROWS_TWO :, :] = jnp.zeros((ROWS - ROWS_ONE - ROWS_TWO, C1), BF)
    for kx in range(3):
        px, dx = TAP[kx]
        for ky in range(3):
            py, dy = TAP[ky]
            d = nn(u2t_s[px * 2 + py], b_rows(dx, dy, CY)) * SCALE_TWO
            at = ROWS_ONE + (kx * 3 + ky) * 3 * C1
            buf_s[at : at + C1, :] = d[C1:, C2:].astype(BF)
            buf_s[at + C1 : at + 2 * C1, :] = d[0:C1, 0:C2].astype(BF)
            buf_s[at + 2 * C1 : at + 3 * C1, :] = d[C1:, 0:C2].astype(BF)

    for px in range(2):
        for py in range(2):
            for i in range(MX):
                for j in range(0, MY, 2):
                    pair = jnp.concatenate(
                        [u_ref[0, 2 * i + px, 2 * (j + e) + py] for e in range(2)], 0
                    )
                    at = (i * MY + j) * MZ
                    u1t_s[px * 2 + py, :, at : at + 2 * MZ] = pair.T

    for kx in range(3):
        px, dx = TAP[kx]
        for ky in range(3):
            py, dy = TAP[ky]
            total = None
            for i in range(MX):
                at = ((i + dx) * EY + dy) * MZ
                part = nn(
                    u1t_s[px * 2 + py, :, i * own : (i + 1) * own], a_ref[at : at + own, :]
                )
                total = part if total is None else total + part
            d = total * SCALE_ONE
            at = (kx * 3 + ky) * 3 * CIN
            buf_s[at : at + CIN, :] = d[CIN:, C1:].astype(BF)
            buf_s[at + CIN : at + 2 * CIN, :] = d[0:CIN, 0:C1].astype(BF)
            buf_s[at + 2 * CIN : at + 3 * CIN, :] = d[CIN:, 0:C1].astype(BF)

    core = core_ref[0]
    keep_ref[...] = buf_s[pl.ds(pl.multiple_of(core * HALF, HALF), HALF), :]
    send_ref[...] = buf_s[pl.ds(pl.multiple_of((1 - core) * HALF, HALF), HALF), :]


def input_kernel(a_ref, w1_ref, out_ref, r1_s):
    zero = jnp.zeros((CIN, C1), BF)
    for kx in range(3):
        for ky in range(3):
            at = SLOT[ky] * 2 * CIN
            r1_s[kx, at : at + CIN, 0:C1] = w1_ref[kx, ky, 1]
            r1_s[kx, at : at + CIN, C1:] = zero
            r1_s[kx, at + CIN : at + 2 * CIN, 0:C1] = w1_ref[kx, ky, 2]
            r1_s[kx, at + CIN : at + 2 * CIN, C1:] = w1_ref[kx, ky, 0]
    wide = 2 * CIN
    step = 4
    for i in range(MX):
        for px in range(2):
            for j in range(0, MY, step):
                both = None
                odd = None
                for kx, dx in TAPS[px]:
                    at = ((i + dx) * EY + j) * MZ
                    part = nt(a_ref[at : at + step * MZ, :], r1_s[kx, 0 : 2 * wide, :])
                    both = part if both is None else both + part
                    part = nt(a_ref[at + MZ : at + (step + 1) * MZ, :], r1_s[kx, 2 * wide :, :])
                    odd = part if odd is None else odd + part
                even = both[:, 0:wide].astype(BF)
                odd = (both[:, wide:] + odd).astype(BF)
                for e in range(step):
                    rows = slice(e * MZ, (e + 1) * MZ)
                    out_ref[0, 2 * i + px, 2 * (j + e)] = even[rows]
                    out_ref[0, 2 * i + px, 2 * (j + e) + 1] = odd[rows]


def vmem(n):
    return [pl.BlockSpec(memory_space=pltpu.VMEM)] * n


def main_call(core, u, pre, og, hx, hy, hc, w1, w2):
    return pl.pallas_call(
        main_kernel,
        out_shape=(
            jax.ShapeDtypeStruct((EX * EY * MZ, 2 * C1), BF),
            jax.ShapeDtypeStruct((HALF, C1), BF),
            jax.ShapeDtypeStruct((HALF, C1), BF),
        ),
        in_specs=[pl.BlockSpec(memory_space=pltpu.SMEM)] + vmem(8),
        out_specs=tuple(vmem(3)),
        scratch_shapes=[
            pltpu.VMEM((2 * (CY + 1) * CZ, 2 * C2), BF),
            pltpu.VMEM((9, 2 * C1, 2 * C2), BF),
            pltpu.VMEM((EX * EY * MZ, C1), F32),
            pltpu.VMEM((MX * MY * MZ, C1), F32),
            pltpu.VMEM((4, 2 * C1, CY * CZ), BF),
            pltpu.VMEM((4, 2 * CIN, MX * MY * MZ), BF),
            pltpu.VMEM((ROWS, C1), BF),
        ],
        cost_estimate=pl.CostEstimate(flops=2_000_000_000, bytes_accessed=8_000_000, transcendentals=0),
        name="main",
    )(core, u, pre, og, hx, hy, hc, w1, w2)


def input_call(a, w1):
    return pl.pallas_call(
        input_kernel,
        out_shape=jax.ShapeDtypeStruct((1, 2 * MX, 2 * MY, MZ, 2 * CIN), BF),
        in_specs=vmem(2),
        out_specs=vmem(1)[0],
        scratch_shapes=[pltpu.VMEM((3, 6 * CIN, 2 * C1), BF)],
        cost_estimate=pl.CostEstimate(flops=1_200_000_000, bytes_accessed=3_000_000, transcendentals=0),
        name="grad_input",
    )(a, w1)


def on_device(u, pre, og, w1, w2):
    core = lax.axis_index("core")
    sx = lax.axis_size("y") * lax.axis_size("xl")
    sz = lax.axis_size("zh") * lax.axis_size("zl")
    AX, AZ = ("y", "xl"), ("zh", "zl")
    from_x = [(i + 1, i) for i in range(sx - 1)]
    from_z = [(i + 1, i) for i in range(sz - 1)]
    from_xz = [
        ((i + 1) * sz + j + 1, i * sz + j) for i in range(sx - 1) for j in range(sz - 1)
    ]
    flat_pre = pre[0].reshape(MX, MY, MZ, C1)
    flat_og = og[0, 0]
    hx = jnp.concatenate([flat_og.reshape(-1, C2), flat_pre[0].reshape(-1, C1)], 0)
    hy = jnp.concatenate([flat_og[0], flat_pre[:, 0].reshape(-1, C1)], 0)
    hc = jnp.concatenate([flat_og[0], flat_pre[0, 0]], 0)
    hx = lax.ppermute(hx, AX, from_x)
    hy = lax.ppermute(hy, AZ, from_z)
    hc = lax.ppermute(hc, AX + AZ, from_xz)
    a, keep, send = main_call(core.reshape(1), u, pre, og, hx, hy, hc, w1, w2)
    received = lax.ppermute(send, "core", [(0, 1), (1, 0)])
    grad_input = input_call(a, w1)

    group = ("xh", "y", "xl", "zl")
    half = (keep.astype(F32) + received.astype(F32)).astype(BF).reshape(GROUP, CHUNK, C1)
    parts = lax.all_to_all(half, group, 0, 0, tiled=True)
    chunk = jnp.sum(parts.astype(F32), axis=0).astype(BF)
    parts = lax.all_to_all(jnp.broadcast_to(chunk[None], (4, CHUNK, C1)), "zh", 0, 0, tiled=True)
    chunk = jnp.sum(parts.astype(F32), axis=0).astype(BF)
    mine = lax.all_to_all(jnp.broadcast_to(chunk[None], (GROUP, CHUNK, C1)), group, 0, 0, tiled=True)
    mine = mine.reshape(HALF, C1)
    other = lax.ppermute(mine, "core", [(0, 1), (1, 0)])
    low = jnp.where(core == 0, mine, other).astype(F32)
    high = jnp.where(core == 0, other, mine).astype(F32)
    grad_one = low[:ROWS_ONE].reshape(3, 3, 3, CIN, C1)
    grad_two = jnp.concatenate([low[ROWS_ONE:], high[: ROWS_ONE + ROWS_TWO - HALF]], 0)
    return grad_input, grad_one, grad_two.reshape(3, 3, 3, C1, C2)


def solution(mesh):
    fine = Mesh(mesh.devices.reshape(2, 2, 4, 2, 4, 2), ("xh", "core", "y", "xl", "zh", "zl"))
    spec = P(("xh", "core"), ("y", "xl"), ("zh", "zl"), None, None)
    return jax.shard_map(
        on_device,
        mesh=fine,
        in_specs=(spec, spec, spec, P(), P()),
        out_specs=(spec, P(), P()),
        check_vma=False,
    )
```

time: 413 us -> 89.3 us (0.22)
  waiting for transfers between devices: 265 us -> 8.73 us
  local copies, waits for them, and re-layouts: 67.6 us -> 4.88 us
  blocking collectives: 0 us -> 51.4 us
  matrix products: 24.9 us -> 0 us
  between operations: 15.7 us -> 0.72 us
  starting transfers between devices: 23.4 us -> 11.1 us
  other arithmetic: 13 us -> 3.76 us
  Pallas kernels: 0 us -> 8.01 us
    psum x1 -> x0, waiting for transfers between devices: 264 us -> none  [on_device(): grad_one, grad_two = lax.psum((grad_one, grad_two), ('dp', 'sx', 'syz'))]
    unnamed x223 -> x6, local copies, waits for them, and re-layouts: 54.1 us -> 0.67 us
    all_to_all x0 -> x3, blocking collectives: none -> 51.4 us  [the longest x1 21.2 us: on_device(): parts = lax.all_to_all(half, group, 0, 0, tiled=True)]
    dot_general x54 -> x0, matrix products: 24.9 us -> none  [the longest x18 16.9 us: data_grad(): jnp.einsum('xyzk,kc->xyzc', window, matrix, preferred_element_type=jnp.fl...]
    ppermute x8 -> x5, starting transfers between devices: 23.4 us -> 11.1 us  [the longest x1 3.65 us: on_device(): other = lax.ppermute(mine, 'core', [(0, 1), (1, 0)])]
    pallas_call x0 -> x2, Pallas kernels: none -> 8.01 us  [the longest x1 4.74 us: main_call(): pl.pallas_call(main_kernel, out_shape=(jax.ShapeDtypeStruct((EX * EY * MZ...]
    ppermute x8 -> x5, waiting for transfers between devices: 0.82 us -> 8.73 us  [the longest x1 6.7 us: on_device(): hc = lax.ppermute(hc, AX + AZ, from_xz)]
    slice x18 -> x4, local copies, waits for them, and re-layouts: 9.37 us -> 2.68 us  [the longest x1 0.97 us: on_device(): grad_one = low[:ROWS_ONE].reshape(3, 3, 3, CIN, C1)]
  transfers between devices with their start and end apart: 9 -> 5, of which waited for: 2 -> 2; matrix products, arithmetic and copies ran while one was open for 21% -> 3% of each run, Pallas kernels for 0% -> 4%
where the time goes in v1:
time: 89.3 us; the launch traced here: 88.6 us
  blocking collectives  51.4 us (58%)
  starting transfers between devices  11.1 us (12%)
  waiting for transfers between devices  8.73 us (10%)
  Pallas kernels  8.01 us (9%)
  local copies, waits for them, and re-layouts  4.88 us (5%)
  other arithmetic  3.76 us (4%)
    all_to_all x1, blocking collectives, on_device(): parts = lax.all_to_all(half, group, 0, 0, tiled=True)  21.2 us
    all_to_all x1, blocking collectives, on_device(): lax.all_to_all(jnp.broadcast_to(chunk[None], (GROUP, CHUNK, C1)), group,...  15.2 us
    all_to_all x1, blocking collectives, on_device(): lax.all_to_all(jnp.broadcast_to(chunk[None], (4, CHUNK, C1)), 'zh', 0, 0,...  15 us
    ppermute x1, waiting for transfers between devices, on_device(): hc = lax.ppermute(hc, AX + AZ, from_xz)  6.7 us
    pallas_call x1, Pallas kernels, main_call(): pl.pallas_call(main_kernel, out_shape=(jax.ShapeDtypeStruct((EX * EY * MZ...  4.74 us
    ppermute x1, starting transfers between devices, on_device(): other = lax.ppermute(mine, 'core', [(0, 1), (1, 0)])  3.65 us
    ppermute x1, starting transfers between devices, on_device(): received = lax.ppermute(send, 'core', [(0, 1), (1, 0)])  3.63 us
    pallas_call x1, Pallas kernels, input_call(): pl.pallas_call(input_kernel, out_shape=jax.ShapeDtypeStruct((1, 2 * MX, 2...  3.27 us
  transfers between devices with their start and end apart: 5, of which 2 were waited for; matrix products, arithmetic and copies ran while one was open for 3% of the time, Pallas kernels for 4%

profile of v1, /device:TPU:1, one launch (start us, length us, event | category | flops | bytes accessed | tf_op | source)
XLA Modules:
  0.0 88.6 jit_solution(667267172910854082)
XLA Ops:
  0.6 0.7 slice_bitcast_fusion.1
  1.3 0.8 slice.35
  2.1 1.3 %collective-permute-start.1 = (bf16[160,128]{1,0:T(8,128)(2,1)S(1)}, bf16[160,128]{1,0:T(8,128)(2,1)S(1)}, u32[]{:S(2)}, u32[]{:S(2)}) collective-permute-start(bf16[160,128]{1,0:T(8,128)(2,1)S(1)} %pad_maximum_fusion.2), channel_id=1, source_target_pairs={{1,0},{2,1},{3,2},{4,3},{5,4},{6,5},{7,6},{9,8},{10,9},{11,10},{12... | collective-permute-start | bytes 122888 | tf_op jit(solution)/shard_map/ppermute | solution.py:247
  3.4 0.9 %slice.27 = bf16[1,1,8,64,128]{4,3,2,1,0:T(8,128)(2,1)S(1)} slice(bf16[1,2,8,64,128]{4,3,2,1,0:T(8,128)(2,1)} %pre_ref.1), slice={[0:1], [0:1], [0:8], [0:64], [0:128]} | slice | bytes 262144 | tf_op jit(solution)/shard_map/slice | solution.py:243
  4.3 0.8 pad_maximum_fusion.1
  5.1 1.3 %collective-permute-start = (bf16[640,128]{1,0:T(8,128)(2,1)S(1)}, bf16[640,128]{1,0:T(8,128)(2,1)S(1)}, u32[]{:S(2)}, u32[]{:S(2)}) collective-permute-start(bf16[640,128]{1,0:T(8,128)(2,1)S(1)} %pad_maximum_fusion.1), channel_id=1, source_target_pairs={{8,0},{16,8},{24,16},{32,24},{40,32},{48,40},{56,48},{9,1},{17,9},... | collective-permute-start | bytes 491528 | tf_op jit(solution)/shard_map/ppermute | solution.py:246
  6.4 0.7 slice_bitcast_fusion
  7.1 1.3 %collective-permute-start.2 = (bf16[96,128]{1,0:T(8,128)(2,1)S(1)}, bf16[96,128]{1,0:T(8,128)(2,1)S(1)}, u32[]{:S(2)}, u32[]{:S(2)}) collective-permute-start(bf16[96,128]{1,0:T(8,128)(2,1)S(1)} %pad_maximum_fusion.3), channel_id=1, source_target_pairs={{9,0},{10,1},{11,2},{12,3},{13,4},{14,5},{15,6},{17,8},{18,9},{19,... | collective-permute-start | bytes 73736 | tf_op jit(solution)/shard_map/ppermute | solution.py:248
  8.4 6.7 %collective-permute-done.2.hc_ref = bf16[96,128]{1,0:T(8,128)(2,1)S(1)} collective-permute-done((bf16[96,128]{1,0:T(8,128)(2,1)S(1)}, bf16[96,128]{1,0:T(8,128)(2,1)S(1)}, u32[]{:S(2)}, u32[]{:S(2)}) %collective-permute-start.2) | collective-permute-done | bytes 24608 | tf_op jit(solution)/shard_map/ppermute | solution.py:248
  15.1 0.0 copy-start.2
  15.1 0.0 collective-permute-done.1.hy_ref
  15.1 0.0 collective-permute-done.hx_ref
  15.1 0.0 copy-start
  15.1 0.6 copy-done.2
  15.7 0.0 copy-done.1
  15.7 0.1 copy-done
  15.8 4.7 %main.1 = (bf16[1728,256]{1,0:T(8,128)(2,1)}, bf16[2816,128]{1,0:T(8,128)(2,1)}, bf16[2816,128]{1,0:T(8,128)(2,1)}) custom-call(s32[1]{0:T(128)} %bitcast.core_ref, bf16[1,4,16,64,128]{4,3,2,1,0:T(8,128)(2,1)} %u_ref.1, bf16[1,2,8,64,128]{4,3,2,1,0:T(8,128)(2,1)} %pre_ref.1, bf16[1,1,4,32,128]{4,3,2,1,0:T(8,128)(2,1)} %og_ref.1, bf16[640,128]{1,0:T(8,128)(2,1)} %copy-done, ...), custom_call_target="tpu_custom_call" | custom-call | flops 2000000000 | bytes 8000000 | tf_op jit(solution)/shard_map/main/pallas_call | solution.py:196
  20.5 3.6 %collective-permute-start.3 = (bf16[2816,128]{1,0:T(8,128)(2,1)}, bf16[2816,128]{1,0:T(8,128)(2,1)S(1)}, u32[]{:S(2)}, u32[]{:S(2)}) collective-permute-start(bf16[2816,128]{1,0:T(8,128)(2,1)} %get-tuple-element.8), channel_id=1, source_target_pairs={{0,64},{64,0},{1,65},{65,1},{2,66},{66,2},{3,67},{67,3},{4,68},{68... | collective-permute-start | bytes 2162696 | tf_op jit(solution)/shard_map/ppermute | solution.py:250
  24.2 2.0 %collective-permute-done.3 = bf16[2816,128]{1,0:T(8,128)(2,1)S(1)} collective-permute-done((bf16[2816,128]{1,0:T(8,128)(2,1)}, bf16[2816,128]{1,0:T(8,128)(2,1)S(1)}, u32[]{:S(2)}, u32[]{:S(2)}) %collective-permute-start.3) | collective-permute-done | bytes 720928 | tf_op jit(solution)/shard_map/ppermute | solution.py:250
  26.2 1.3 %add_convert_fusion = bf16[2816,128]{1,0:T(8,128)(2,1)S(1)} fusion(bf16[2816,128]{1,0:T(8,128)(2,1)S(1)} %collective-permute-done.3, bf16[2816,128]{1,0:T(8,128)(2,1)} %get-tuple-element.7), kind=kLoop, calls=%fused_computation.1 | loop fusion | flops 1441792 | bytes 2162688 | tf_op jit(solution)/shard_map/convert_element_type | solution.py:254
  27.5 21.2 %all_to_all.15 = bf16[32,88,128]{2,1,0:T(8,128)(2,1)S(1)} all-to-all(bf16[32,88,128]{2,1,0:T(8,128)(2,1)S(1)} %bitcast.16), channel_id=1, replica_groups=mesh['xh'=2,'core'=2,'y'=4,'xl'=2,'zh'=4,'zl'=2] {'xh','y','xl','zl'}, dimensions={0} | all-to-all | bytes 1441792 | tf_op jit(solution)/shard_map/all_to_all | solution.py:255
  48.7 0.1 reduce_sum.24
  48.9 15.0 %all_to_all.16 = bf16[4,88,128]{2,1,0:T(8,128)(2,1)S(1)} all-to-all(bf16[4,88,128]{2,1,0:T(8,128)(2,1)S(1)} %broadcast_in_dim.4), channel_id=1, replica_groups=mesh['xh'=2,'core'=2,'y'=4,'xl'=2,'zh'=4,'zl'=2] {'zh'}, dimensions={0} | all-to-all | bytes 180224 | tf_op jit(solution)/shard_map/all_to_all | solution.py:257
  63.9 0.1 broadcast_in_dim.5
  64.0 15.2 %all_to_all.17 = bf16[32,88,128]{2,1,0:T(8,128)(2,1)S(1)} all-to-all(bf16[32,88,128]{2,1,0:T(8,128)(2,1)S(1)} %broadcast_in_dim.5), channel_id=1, replica_groups=mesh['xh'=2,'core'=2,'y'=4,'xl'=2,'zh'=4,'zl'=2] {'xh','y','xl','zl'}, dimensions={0} | all-to-all | bytes 1441792 | tf_op jit(solution)/shard_map/all_to_all | solution.py:259
  79.1 3.7 %collective-permute-start.4 = (bf16[2816,128]{1,0:T(8,128)(2,1)S(1)}, bf16[2816,128]{1,0:T(8,128)(2,1)S(1)}, u32[]{:S(2)}, u32[]{:S(2)}) collective-permute-start(bf16[2816,128]{1,0:T(8,128)(2,1)S(1)} %bitcast.14), channel_id=1, source_target_pairs={{0,64},{64,0},{1,65},{65,1},{2,66},{66,2},{3,67},{67,3},{4,68},{68... | collective-permute-start | bytes 2162696 | tf_op jit(solution)/shard_map/ppermute | solution.py:261
  82.8 3.3 %grad_input.1 = bf16[1,4,16,64,128]{4,3,2,1,0:T(8,128)(2,1)} custom-call(bf16[1728,256]{1,0:T(8,128)(2,1)} %get-tuple-element.6.a_ref, bf16[3,3,3,64,128]{4,3,2,1,0:T(8,128)(2,1)} %w1_ref.3), custom_call_target="tpu_custom_call" | custom-call | flops 1200000000 | bytes 3000000 | tf_op jit(solution)/shard_map/grad_input/pallas_call | solution.py:220
  86.1 0.0 collective-permute-done.4
  86.1 0.1 select_convert_fusion
  86.3 1.0 %slice.37 = f32[1728,128]{1,0:T(8,128)} slice(f32[2816,128]{1,0:T(8,128)S(1)} %select_convert_fusion), slice={[0:1728], [0:128]} | slice | bytes 1769472 | tf_op jit(solution)/shard_map/slice | solution.py:264
  87.2 0.1 fusion
  87.3 1.3 %pad_maximum_fusion = f32[3456,128]{1,0:T(8,128)} fusion(f32[2368,128]{1,0:T(8,128)S(1)} %fusion, f32[1088,128]{1,0:T(8,128)S(1)} %slice.38), kind=kLoop, calls=%fused_computation | loop fusion | flops 442368 | bytes 3538944 | tf_op jit(solution)/shard_map/concatenate | solution.py:265
  (6 shorter events, 0.1 us)
Async XLA Ops:
  2.1 13.0 %collective-permute-start.1 = (bf16[160,128]{1,0:T(8,128)(2,1)S(1)}, bf16[160,128]{1,0:T(8,128)(2,1)S(1)}, u32[]{:S(2)}, u32[]{:S(2)}) collective-permute-start(bf16[160,128]{1,0:T(8,128)(2,1)S(1)} %pad_maximum_fusion.2), channel_id=1, source_target_pairs={{1,0},{2,1},{3,2},{4,3},{5,4},{6,5},{7,6},{9,8},{10,9},{11,10},{12... | collective-permute-start | bytes 122888 | tf_op jit(solution)/shard_map/ppermute | solution.py:247
  5.1 10.0 %collective-permute-start = (bf16[640,128]{1,0:T(8,128)(2,1)S(1)}, bf16[640,128]{1,0:T(8,128)(2,1)S(1)}, u32[]{:S(2)}, u32[]{:S(2)}) collective-permute-start(bf16[640,128]{1,0:T(8,128)(2,1)S(1)} %pad_maximum_fusion.1), channel_id=1, source_target_pairs={{8,0},{16,8},{24,16},{32,24},{40,32},{48,40},{56,48},{9,1},{17,9},... | collective-permute-start | bytes 491528 | tf_op jit(solution)/shard_map/ppermute | solution.py:246
  7.1 8.0 %collective-permute-start.2 = (bf16[96,128]{1,0:T(8,128)(2,1)S(1)}, bf16[96,128]{1,0:T(8,128)(2,1)S(1)}, u32[]{:S(2)}, u32[]{:S(2)}) collective-permute-start(bf16[96,128]{1,0:T(8,128)(2,1)S(1)} %pad_maximum_fusion.3), channel_id=1, source_target_pairs={{9,0},{10,1},{11,2},{12,3},{13,4},{14,5},{15,6},{17,8},{18,9},{19,... | collective-permute-start | bytes 73736 | tf_op jit(solution)/shard_map/ppermute | solution.py:248
  15.1 0.6 copy-start.2
  15.1 0.6 copy-start.1
  15.1 0.7 copy-start
  20.5 5.7 %collective-permute-start.3 = (bf16[2816,128]{1,0:T(8,128)(2,1)}, bf16[2816,128]{1,0:T(8,128)(2,1)S(1)}, u32[]{:S(2)}, u32[]{:S(2)}) collective-permute-start(bf16[2816,128]{1,0:T(8,128)(2,1)} %get-tuple-element.8), channel_id=1, source_target_pairs={{0,64},{64,0},{1,65},{65,1},{2,66},{66,2},{3,67},{67,3},{4,68},{68... | collective-permute-start | bytes 2162696 | tf_op jit(solution)/shard_map/ppermute | solution.py:250
  79.1 6.9 %collective-permute-start.4 = (bf16[2816,128]{1,0:T(8,128)(2,1)S(1)}, bf16[2816,128]{1,0:T(8,128)(2,1)S(1)}, u32[]{:S(2)}, u32[]{:S(2)}) collective-permute-start(bf16[2816,128]{1,0:T(8,128)(2,1)S(1)} %bitcast.14), channel_id=1, source_target_pairs={{0,64},{64,0},{1,65},{65,1},{2,66},{66,2},{3,67},{67,3},{4,68},{68... | collective-permute-start | bytes 2162696 | tf_op jit(solution)/shard_map/ppermute | solution.py:261

commit v2 on v1

v2 whole, which is shorter than its diff:
```python
import functools

import jax
import jax.numpy as jnp
from jax import lax
from jax.experimental import pallas as pl
from jax.experimental.pallas import tpu as pltpu
from jax.sharding import Mesh
from jax.sharding import PartitionSpec as P

BF = jnp.bfloat16
F32 = jnp.float32

CX, CY, CZ = 1, 4, 32
MX, MY, MZ = 2, 8, 64
CIN, C1, C2 = 64, 128, 128
EX, EY = MX + 1, MY + 1
CHUNK = 88
GROUP = 32
HALF = CHUNK * GROUP
ROWS_ONE = 27 * CIN
ROWS_TWO = 27 * C1
ROWS = 2 * HALF
SCALE_ONE = float(4 * 16 * 64 * 64) ** (-0.5)
SCALE_TWO = float(4 * 8 * 32 * 32) ** (-0.5)

TAP = ((1, 1), (0, 0), (1, 0))
TAPS = (((1, 0),), ((2, 0), (0, 1)))
SLOT = (2, 0, 1)


def nt(a, b):
    return lax.dot_general(a, b, (((1,), (1,)), ((), ())), preferred_element_type=F32)


def nn(a, b):
    return lax.dot_general(a, b, (((1,), (0,)), ((), ())), preferred_element_type=F32)


def next_row(value, period):
    rows = value.shape[0]
    rolled = pltpu.roll(value, rows - 1, 0)
    row = lax.broadcasted_iota(jnp.int32, value.shape, 0)
    return jnp.where(row % period == period - 1, 0.0, rolled)


def pack_kernel(pre_ref, og_ref, hx_ref, hy_ref, hc_ref, sems):
    copies = []

    def copy(src, dst):
        copies.append(pltpu.make_async_copy(src, dst, sems.at[len(copies)]))
        copies[-1].start()

    for j in range(CY):
        copy(og_ref.at[0, 0, j], hx_ref.at[pl.ds(j * CZ, CZ)])
    for y in range(MY):
        copy(pre_ref.at[0, 0, y], hx_ref.at[pl.ds(CY * CZ + y * MZ, MZ)])
    copy(og_ref.at[0, 0, 0], hy_ref.at[pl.ds(0, CZ)])
    for x in range(MX):
        copy(pre_ref.at[0, x, 0], hy_ref.at[pl.ds(CZ + x * MZ, MZ)])
    copy(og_ref.at[0, 0, 0], hc_ref.at[pl.ds(0, CZ)])
    copy(pre_ref.at[0, 0, 0], hc_ref.at[pl.ds(CZ, MZ)])
    for c in copies:
        c.wait()


def prep_kernel(u_ref, pre_ref, w1_ref, w2_ref, r1_ref, r2_ref, u1t_ref, u2t_ref, act_s):
    zero = jnp.zeros((CIN, C1), BF)
    for kx in range(3):
        for ky in range(3):
            at = SLOT[ky] * 2 * CIN
            r1_ref[kx, at : at + CIN, 0:C1] = w1_ref[kx, ky, 1]
            r1_ref[kx, at : at + CIN, C1:] = zero
            r1_ref[kx, at + CIN : at + 2 * CIN, 0:C1] = w1_ref[kx, ky, 2]
            r1_ref[kx, at + CIN : at + 2 * CIN, C1:] = w1_ref[kx, ky, 0]

    zero = jnp.zeros((C1, C2), BF)
    for kx in range(3):
        for ky in range(3):
            t = kx * 3 + ky
            r2_ref[t, 0:C1, 0:C2] = w2_ref[kx, ky, 1]
            r2_ref[t, 0:C1, C2:] = zero
            r2_ref[t, C1:, 0:C2] = w2_ref[kx, ky, 2]
            r2_ref[t, C1:, C2:] = w2_ref[kx, ky, 0]

    own = MY * MZ
    for mx in range(MX):
        pre = pre_ref[0, mx].reshape(own, C1).astype(F32)
        act_s[mx * own : (mx + 1) * own, :] = jnp.where(pre > 0, pre, 0.3 * pre)
    for px in range(2):
        for py in range(2):
            for s in range(2):
                rows = [
                    act_s[pl.ds((px * MY + 2 * j + py) * MZ + s, CZ, stride=2), :]
                    for j in range(CY)
                ]
                u2t_ref[px * 2 + py, s * C1 : (s + 1) * C1, :] = jnp.concatenate(rows, 0).T.astype(BF)

    for px in range(2):
        for py in range(2):
            for i in range(MX):
                for j in range(0, MY, 2):
                    pair = jnp.concatenate(
                        [u_ref[0, 2 * i + px, 2 * (j + e) + py] for e in range(2)], 0
                    )
                    at = (i * MY + j) * MZ
                    u1t_ref[px * 2 + py, :, at : at + 2 * MZ] = pair.T


def main_kernel(
    core_ref, pre_ref, og_ref, hx_ref, hy_ref, hc_ref, r2_ref, u1t_ref, u2t_ref,
    a_ref, keep_ref, send_ref,
    b_s, ga_s, buf_s,
):
    def put_b(at, value):
        n = value.shape[0]
        b_s[at : at + n, 0:C2] = value
        b_s[at : at + n, C2:] = next_row(value.astype(F32), CZ).astype(BF)

    put_b(0, og_ref[0, 0].reshape(CY * CZ, C2))
    put_b(CY * CZ, hy_ref[0:CZ])
    put_b((CY + 1) * CZ, hx_ref[0 : CY * CZ])
    put_b((2 * CY + 1) * CZ, hc_ref[0:CZ])

    def put_ga(mx, my, value):
        base = (mx * EY + my) * MZ
        ga_s[pl.ds(base, CZ, stride=2), :] = value[:, 0:C1]
        ga_s[pl.ds(base + 1, CZ, stride=2), :] = value[:, C1:]

    def b_rows(i, j, n):
        at = (i * (CY + 1) + j) * CZ
        return b_s[at : at + n * CZ, :]

    for px in range(2):
        for i in range(2 - px):
            for py in range(2):
                n = CY + 1 - py
                total = None
                for kx, dx in TAPS[px]:
                    for ky, dy in TAPS[py]:
                        part = nt(b_rows(i + dx, dy, n), r2_ref[kx * 3 + ky])
                        total = part if total is None else total + part
                for j in range(n):
                    put_ga(2 * i + px, 2 * j + py, total[j * CZ : (j + 1) * CZ])

    def put_a(at, pre):
        n = pre.shape[0]
        slope = jnp.where(pre.astype(F32) > 0, 1.0, 0.3)
        value = ga_s[at : at + n, :] * slope
        a_ref[at : at + n, 0:C1] = value.astype(BF)
        a_ref[at : at + n, C1:] = next_row(value, MZ).astype(BF)

    own = MY * MZ
    for mx in range(MX):
        put_a(mx * EY * MZ, pre_ref[0, mx].reshape(own, C1))
        put_a((mx * EY + MY) * MZ, hy_ref[CZ + mx * MZ : CZ + (mx + 1) * MZ])
    put_a(MX * EY * MZ, hx_ref[CY * CZ : CY * CZ + own])
    put_a((MX * EY + MY) * MZ, hc_ref[CZ : CZ + MZ])

    buf_s[ROWS_ONE + ROWS_TWO :, :] = jnp.zeros((ROWS - ROWS_ONE - ROWS_TWO, C1), BF)
    for kx in range(3):
        px, dx = TAP[kx]
        for ky in range(3):
            py, dy = TAP[ky]
            d = nn(u2t_ref[px * 2 + py], b_rows(dx, dy, CY)) * SCALE_TWO
            at = ROWS_ONE + (kx * 3 + ky) * 3 * C1
            buf_s[at : at + C1, :] = d[C1:, C2:].astype(BF)
            buf_s[at + C1 : at + 2 * C1, :] = d[0:C1, 0:C2].astype(BF)
            buf_s[at + 2 * C1 : at + 3 * C1, :] = d[C1:, 0:C2].astype(BF)

    for kx in range(3):
        px, dx = TAP[kx]
        for ky in range(3):
            py, dy = TAP[ky]
            total = None
            for i in range(MX):
                at = ((i + dx) * EY + dy) * MZ
                part = nn(
                    u1t_ref[px * 2 + py, :, i * own : (i + 1) * own], a_ref[at : at + own, :]
                )
                total = part if total is None else total + part
            d = total * SCALE_ONE
            at = (kx * 3 + ky) * 3 * CIN
            buf_s[at : at + CIN, :] = d[CIN:, C1:].astype(BF)
            buf_s[at + CIN : at + 2 * CIN, :] = d[0:CIN, 0:C1].astype(BF)
            buf_s[at + 2 * CIN : at + 3 * CIN, :] = d[CIN:, 0:C1].astype(BF)

    core = core_ref[0]
    keep_ref[...] = buf_s[pl.ds(pl.multiple_of(core * HALF, HALF), HALF), :]
    send_ref[...] = buf_s[pl.ds(pl.multiple_of((1 - core) * HALF, HALF), HALF), :]


def input_kernel(a_ref, r1_ref, out_ref):
    wide = 2 * CIN
    step = 4
    for i in range(MX):
        for px in range(2):
            for j in range(0, MY, step):
                both = None
                odd = None
                for kx, dx in TAPS[px]:
                    at = ((i + dx) * EY + j) * MZ
                    part = nt(a_ref[at : at + step * MZ, :], r1_ref[kx, 0 : 2 * wide, :])
                    both = part if both is None else both + part
                    part = nt(a_ref[at + MZ : at + (step + 1) * MZ, :], r1_ref[kx, 2 * wide :, :])
                    odd = part if odd is None else odd + part
                even = both[:, 0:wide].astype(BF)
                odd = (both[:, wide:] + odd).astype(BF)
                for e in range(step):
                    rows = slice(e * MZ, (e + 1) * MZ)
                    out_ref[0, 2 * i + px, 2 * (j + e)] = even[rows]
                    out_ref[0, 2 * i + px, 2 * (j + e) + 1] = odd[rows]


def output_kernel(core_ref, mine_ref, other_ref, one_ref, two_ref):
    low = HALF - ROWS_ONE
    high = ROWS_TWO - low

    def put(first_ref, second_ref):
        one_ref[...] = first_ref[0:ROWS_ONE].astype(F32)
        two_ref[0:low] = first_ref[ROWS_ONE:].astype(F32)
        two_ref[low:] = second_ref[0:high].astype(F32)

    @pl.when(core_ref[0] == 0)
    def _():
        put(mine_ref, other_ref)

    @pl.when(core_ref[0] != 0)
    def _():
        put(other_ref, mine_ref)


def vmem(n):
    return [pl.BlockSpec(memory_space=pltpu.VMEM)] * n


def near(x):
    return pltpu.with_memory_space_constraint(x, pltpu.VMEM)


SMEM = pl.BlockSpec(memory_space=pltpu.SMEM)
LIMIT = 20 * 1024 * 1024


def call(kernel, name, out, scratch, in_specs, flops, bytes_moved):
    return pl.pallas_call(
        kernel,
        out_shape=tuple(out),
        in_specs=in_specs,
        out_specs=tuple(vmem(len(out))),
        scratch_shapes=scratch,
        cost_estimate=pl.CostEstimate(flops=flops, bytes_accessed=bytes_moved, transcendentals=0),
        compiler_params=pltpu.CompilerParams(vmem_limit_bytes=LIMIT),
        name=name,
    )


def pack_call(pre, og):
    out = [pltpu.VMEM(((CY * CZ + MY * MZ), C1), BF), pltpu.VMEM((CZ + MX * MZ, C1), BF), pltpu.VMEM((CZ + MZ, C1), BF)]
    count = CY + MY + 1 + MX + 2
    any_spec = [pl.BlockSpec(memory_space=pl.ANY)] * 2
    return call(pack_kernel, "pack", out, [pltpu.SemaphoreType.DMA((count,))], any_spec, 0, 500_000)(pre, og)


def prep_call(u, pre, w1, w2):
    out = [
        pltpu.VMEM((3, 6 * CIN, 2 * C1), BF),
        pltpu.VMEM((9, 2 * C1, 2 * C2), BF),
        pltpu.VMEM((4, 2 * CIN, MX * MY * MZ), BF),
        pltpu.VMEM((4, 2 * C1, CY * CZ), BF),
    ]
    scratch = [pltpu.VMEM((MX * MY * MZ, C1), F32)]
    return call(prep_kernel, "prep", out, scratch, vmem(4), 0, 6_000_000)(u, pre, w1, w2)


def main_call(core, pre, og, hx, hy, hc, r2, u1t, u2t):
    out = [
        pltpu.VMEM((EX * EY * MZ, 2 * C1), BF),
        pltpu.VMEM((HALF, C1), BF),
        pltpu.VMEM((HALF, C1), BF),
    ]
    scratch = [
        pltpu.VMEM((2 * (CY + 1) * CZ, 2 * C2), BF),
        pltpu.VMEM((EX * EY * MZ, C1), F32),
        pltpu.VMEM((ROWS, C1), BF),
    ]
    return call(main_kernel, "main", out, scratch, [SMEM] + vmem(8), 2_000_000_000, 8_000_000)(
        core, pre, og, hx, hy, hc, r2, u1t, u2t
    )


def input_call(a, r1):
    out = [jax.ShapeDtypeStruct((1, 2 * MX, 2 * MY, MZ, 2 * CIN), BF)]
    return call(input_kernel, "grad_input", out, [], vmem(2), 1_200_000_000, 3_000_000)(a, r1)[0]


def output_call(core, mine, other):
    out = [jax.ShapeDtypeStruct((ROWS_ONE, C1), F32), jax.ShapeDtypeStruct((ROWS_TWO, C1), F32)]
    return call(output_kernel, "output", out, [], [SMEM] + vmem(2), 0, 4_000_000)(core, mine, other)


def on_device(u, pre, og, w1, w2):
    core = lax.axis_index("core").reshape(1)
    sx = lax.axis_size("y") * lax.axis_size("xl")
    sz = lax.axis_size("zh") * lax.axis_size("zl")
    AX, AZ = ("y", "xl"), ("zh", "zl")
    from_x = [(i + 1, i) for i in range(sx - 1)]
    from_z = [(i + 1, i) for i in range(sz - 1)]
    from_xz = [
        ((i + 1) * sz + j + 1, i * sz + j) for i in range(sx - 1) for j in range(sz - 1)
    ]
    hx, hy, hc = pack_call(pre, og)
    hx = lax.ppermute(hx, AX, from_x)
    hc = lax.ppermute(hc, AX + AZ, from_xz)
    hy = lax.ppermute(hy, AZ, from_z)
    r1, r2, u1t, u2t = prep_call(u, pre, w1, w2)
    a, keep, send = main_call(core, pre, og, hx, hy, hc, r2, u1t, u2t)
    received = lax.ppermute(send, "core", [(0, 1), (1, 0)])
    grad_input = input_call(a, r1)

    group = ("xh", "y", "xl", "zl")
    half = (keep.astype(F32) + received.astype(F32)).astype(BF).reshape(GROUP, CHUNK, C1)
    parts = lax.all_to_all(half, group, 0, 0, tiled=True)
    chunk = jnp.sum(parts.astype(F32), axis=0).astype(BF)
    parts = lax.all_to_all(jnp.broadcast_to(chunk[None], (4, CHUNK, C1)), "zh", 0, 0, tiled=True)
    chunk = jnp.sum(parts.astype(F32), axis=0).astype(BF)
    mine = lax.all_to_all(jnp.broadcast_to(chunk[None], (GROUP, CHUNK, C1)), group, 0, 0, tiled=True)
    mine = mine.reshape(HALF, C1)
    other = lax.ppermute(mine, "core", [(0, 1), (1, 0)])
    grad_one, grad_two = output_call(core, mine, other)
    return grad_input, grad_one.reshape(3, 3, 3, CIN, C1), grad_two.reshape(3, 3, 3, C1, C2)


def solution(mesh):
    fine = Mesh(mesh.devices.reshape(2, 2, 4, 2, 4, 2), ("xh", "core", "y", "xl", "zh", "zl"))
    spec = P(("xh", "core"), ("y", "xl"), ("zh", "zl"), None, None)
    return jax.shard_map(
        on_device,
        mesh=fine,
        in_specs=(spec, spec, spec, P(), P()),
        out_specs=(spec, P(), P()),
        check_vma=False,
    )
```

time: 89.3 us -> 81 us (0.907)
  waiting for transfers between devices: 8.73 us -> 3.48 us
  other arithmetic: 3.76 us -> 0.32 us
  Pallas kernels: 8.01 us -> 6.62 us
  local copies, waits for them, and re-layouts: 4.88 us -> 6.16 us
    unnamed x6 -> x14, local copies, waits for them, and re-layouts: 0.67 us -> 6.06 us
    ppermute x1, waiting for transfers between devices: 6.7 us -> 1.65 us  [on_device(): hc = lax.ppermute(hc, AX + AZ, from_xz)]
    slice x4 -> x0, local copies, waits for them, and re-layouts: 2.68 us -> none  [the longest x1 0.97 us: on_device(): grad_one = low[:ROWS_ONE].reshape(3, 3, 3, CIN, C1)]
    concatenate x4 -> x0, other arithmetic: 2.11 us -> none  [the longest x1 1.32 us: on_device(): jnp.concatenate([low[ROWS_ONE:], high[:ROWS_ONE + ROWS_TWO - HALF]], 0)]
    squeeze x2 -> x0, local copies, waits for them, and re-layouts: 1.42 us -> none  [the longest x1 0.72 us: on_device(): hc = jnp.concatenate([flat_og[0], flat_pre[0, 0]], 0)]
    pallas_call x2 -> x5, Pallas kernels: 8.01 us -> 6.62 us  [the longest x1 1.97 us: input_call(): call(input_kernel, 'grad_input', out, [], vmem(2), 1200000000, 3000000)]
    convert_element_type x1, other arithmetic: 1.3 us -> 0.19 us  [on_device(): (keep.astype(F32) + received.astype(F32)).astype(BF)]
  transfers between devices with their start and end apart: 5 -> 5, of which waited for: 2 -> 2; matrix products, arithmetic and copies ran while one was open for 3% -> 0% of each run, Pallas kernels for 4% -> 3%
where the time goes in v2:
time: 81 us; the launch traced here: 80.4 us
  blocking collectives  51.9 us (64%)
  starting transfers between devices  11.2 us (14%)
  Pallas kernels  6.62 us (8%)
  local copies, waits for them, and re-layouts  6.16 us (8%)
  waiting for transfers between devices  3.48 us (4%)
    all_to_all x1, blocking collectives, on_device(): parts = lax.all_to_all(half, group, 0, 0, tiled=True)  21.4 us
    all_to_all x1, blocking collectives, on_device(): lax.all_to_all(jnp.broadcast_to(chunk[None], (4, CHUNK, C1)), 'zh', 0, 0,...  15.4 us
    all_to_all x1, blocking collectives, on_device(): lax.all_to_all(jnp.broadcast_to(chunk[None], (GROUP, CHUNK, C1)), group,...  15.2 us
    unnamed x14, local copies, waits for them, and re-layouts  6.06 us
    ppermute x1, starting transfers between devices, on_device(): received = lax.ppermute(send, 'core', [(0, 1), (1, 0)])  3.71 us
    ppermute x1, starting transfers between devices, on_device(): other = lax.ppermute(mine, 'core', [(0, 1), (1, 0)])  3.65 us
    pallas_call x1, Pallas kernels, input_call(): call(input_kernel, 'grad_input', out, [], vmem(2), 1200000000, 3000000)  1.97 us
    pallas_call x1, Pallas kernels, main_call(): call(main_kernel, 'main', out, scratch, [SMEM] + vmem(8), 2000000000, 800...  1.84 us
  transfers between devices with their start and end apart: 5, of which 2 were waited for; matrix products, arithmetic and copies ran while one was open for 0% of the time, Pallas kernels for 3%

profile of v2, /device:TPU:1, one launch (start us, length us, event | category | flops | bytes accessed | tf_op | source)
XLA Modules:
  0.0 80.4 jit_solution(2424748594193981768)
XLA Ops:
  0.6 0.0 copy-start
  0.6 0.9 %copy-done = bf16[1,2,8,64,128]{4,3,2,1,0:T(8,128)(2,1)S(1)} copy-done((bf16[1,2,8,64,128]{4,3,2,1,0:T(8,128)(2,1)S(1)}, bf16[1,2,8,64,128]{4,3,2,1,0:T(8,128)(2,1)}, u32[]{:S(2)}) %copy-start) | copy-done | bytes 262168
  1.6 0.0 copy-start.5
  1.6 0.8 copy-done.5
  2.3 0.0 copy-start.6
  2.3 0.5 pack.1
  2.8 1.3 %collective-permute-start = (bf16[640,128]{1,0:T(8,128)(2,1)S(1)}, bf16[640,128]{1,0:T(8,128)(2,1)S(1)}, u32[]{:S(2)}, u32[]{:S(2)}) collective-permute-start(bf16[640,128]{1,0:T(8,128)(2,1)S(1)} %get-tuple-element.15), channel_id=1, source_target_pairs={{8,0},{16,8},{24,16},{32,24},{40,32},{48,40},{56,48},{9,1},{17,9},... | collective-permute-start | bytes 491528 | tf_op jit(solution)/shard_map/ppermute | solution.py:313
  4.1 1.3 %collective-permute-start.1 = (bf16[160,128]{1,0:T(8,128)(2,1)S(1)}, bf16[160,128]{1,0:T(8,128)(2,1)S(1)}, u32[]{:S(2)}, u32[]{:S(2)}) collective-permute-start(bf16[160,128]{1,0:T(8,128)(2,1)S(1)} %get-tuple-element.16), channel_id=1, source_target_pairs={{1,0},{2,1},{3,2},{4,3},{5,4},{6,5},{7,6},{9,8},{10,9},{11,10},{12... | collective-permute-start | bytes 122888 | tf_op jit(solution)/shard_map/ppermute | solution.py:315
  5.4 1.3 %collective-permute-start.2 = (bf16[96,128]{1,0:T(8,128)(2,1)S(1)}, bf16[96,128]{1,0:T(8,128)(2,1)S(1)}, u32[]{:S(2)}, u32[]{:S(2)}) collective-permute-start(bf16[96,128]{1,0:T(8,128)(2,1)S(1)} %get-tuple-element.17), channel_id=1, source_target_pairs={{9,0},{10,1},{11,2},{12,3},{13,4},{14,5},{15,6},{17,8},{18,9},{19,... | collective-permute-start | bytes 73736 | tf_op jit(solution)/shard_map/ppermute | solution.py:314
  6.7 0.0 copy-start.1
  6.7 0.9 %copy-done.1 = bf16[1,2,8,64,128]{4,3,2,1,0:T(8,128)(2,1)S(1)} copy-done((bf16[1,2,8,64,128]{4,3,2,1,0:T(8,128)(2,1)S(1)}, bf16[1,2,8,64,128]{4,3,2,1,0:T(8,128)(2,1)}, u32[]{:S(2)}) %copy-start.1) | copy-done | bytes 262168
  7.7 1.2 %copy-done.2 = bf16[1,4,16,64,128]{4,3,2,1,0:T(8,128)(2,1)S(1)} copy-done((bf16[1,4,16,64,128]{4,3,2,1,0:T(8,128)(2,1)S(1)}, bf16[1,4,16,64,128]{4,3,2,1,0:T(8,128)(2,1)}, u32[]{:S(2)}) %copy-start.2) | copy-done | bytes 1048600
  8.9 1.2 %copy-done.3 = bf16[3,3,3,128,128]{4,3,2,1,0:T(8,128)(2,1)S(1)} copy-done((bf16[3,3,3,128,128]{4,3,2,1,0:T(8,128)(2,1)S(1)}, bf16[3,3,3,128,128]{4,3,2,1,0:T(8,128)(2,1)}, u32[]{:S(2)}) %copy-start.3) | copy-done | bytes 884760
  10.1 1.0 %copy-done.4 = bf16[3,3,3,64,128]{4,3,2,1,0:T(8,128)(2,1)S(1)} copy-done((bf16[3,3,3,64,128]{4,3,2,1,0:T(8,128)(2,1)S(1)}, bf16[3,3,3,64,128]{4,3,2,1,0:T(8,128)(2,1)}, u32[]{:S(2)}) %copy-start.4) | copy-done | bytes 442392
  11.1 0.7 prep.1
  11.8 1.7 %collective-permute-done.2.hc_ref = bf16[96,128]{1,0:T(8,128)(2,1)S(1)} collective-permute-done((bf16[96,128]{1,0:T(8,128)(2,1)S(1)}, bf16[96,128]{1,0:T(8,128)(2,1)S(1)}, u32[]{:S(2)}, u32[]{:S(2)}) %collective-permute-start.2) | collective-permute-done | bytes 24608 | tf_op jit(solution)/shard_map/ppermute | solution.py:314
  13.4 0.0 collective-permute-done.1.hy_ref
  13.4 0.0 collective-permute-done.hx_ref
  13.4 0.0 copy-done.6
  13.4 1.8 %main.1 = (bf16[1728,256]{1,0:T(8,128)(2,1)S(1)}, bf16[2816,128]{1,0:T(8,128)(2,1)S(1)}, bf16[2816,128]{1,0:T(8,128)(2,1)S(1)}) custom-call(s32[1]{0:T(128)} %bitcast.core_ref, bf16[1,2,8,64,128]{4,3,2,1,0:T(8,128)(2,1)S(1)} %copy-done.1, bf16[1,1,4,32,128]{4,3,2,1,0:T(8,128)(2,1)S(1)} %copy-done.6, bf16[640,128]{1,0:T(8,128)(2,1)S(1)} %collective-permute-done.hx_ref, ...), custom_call_target="tpu_custom_call" | custom-call | flops 2000000000 | bytes 8000000 | tf_op jit(solution)/shard_map/main/pallas_call | solution.py:287
  15.3 3.7 %collective-permute-start.3 = (bf16[2816,128]{1,0:T(8,128)(2,1)S(1)}, bf16[2816,128]{1,0:T(8,128)(2,1)S(1)}, u32[]{:S(2)}, u32[]{:S(2)}) collective-permute-start(bf16[2816,128]{1,0:T(8,128)(2,1)S(1)} %get-tuple-element.24), channel_id=1, source_target_pairs={{0,64},{64,0},{1,65},{65,1},{2,66},{66,2},{3,67},{67,3},{4,68},{68... | collective-permute-start | bytes 2162696 | tf_op jit(solution)/shard_map/ppermute | solution.py:318
  19.0 1.8 %collective-permute-done.3 = bf16[2816,128]{1,0:T(8,128)(2,1)S(1)} collective-permute-done((bf16[2816,128]{1,0:T(8,128)(2,1)S(1)}, bf16[2816,128]{1,0:T(8,128)(2,1)S(1)}, u32[]{:S(2)}, u32[]{:S(2)}) %collective-permute-start.3) | collective-permute-done | bytes 720928 | tf_op jit(solution)/shard_map/ppermute | solution.py:318
  20.8 0.2 add_convert_fusion
  21.0 21.4 %all_to_all.15 = bf16[32,88,128]{2,1,0:T(8,128)(2,1)S(1)} all-to-all(bf16[32,88,128]{2,1,0:T(8,128)(2,1)S(1)} %bitcast.7), channel_id=1, replica_groups=mesh['xh'=2,'core'=2,'y'=4,'xl'=2,'zh'=4,'zl'=2] {'xh','y','xl','zl'}, dimensions={0} | all-to-all | bytes 1441792 | tf_op jit(solution)/shard_map/all_to_all | solution.py:323
  42.4 0.1 reduce_sum.24
  42.5 15.4 %all_to_all.16 = bf16[4,88,128]{2,1,0:T(8,128)(2,1)S(1)} all-to-all(bf16[4,88,128]{2,1,0:T(8,128)(2,1)S(1)} %broadcast_in_dim.4), channel_id=1, replica_groups=mesh['xh'=2,'core'=2,'y'=4,'xl'=2,'zh'=4,'zl'=2] {'zh'}, dimensions={0} | all-to-all | bytes 180224 | tf_op jit(solution)/shard_map/all_to_all | solution.py:325
  57.9 0.1 broadcast_in_dim.5
  58.0 15.2 %all_to_all.17 = bf16[32,88,128]{2,1,0:T(8,128)(2,1)S(1)} all-to-all(bf16[32,88,128]{2,1,0:T(8,128)(2,1)S(1)} %broadcast_in_dim.5), channel_id=1, replica_groups=mesh['xh'=2,'core'=2,'y'=4,'xl'=2,'zh'=4,'zl'=2] {'xh','y','xl','zl'}, dimensions={0} | all-to-all | bytes 1441792 | tf_op jit(solution)/shard_map/all_to_all | solution.py:327
  73.1 3.7 %collective-permute-start.4 = (bf16[2816,128]{1,0:T(8,128)(2,1)S(1)}, bf16[2816,128]{1,0:T(8,128)(2,1)S(1)}, u32[]{:S(2)}, u32[]{:S(2)}) collective-permute-start(bf16[2816,128]{1,0:T(8,128)(2,1)S(1)} %bitcast.5), channel_id=1, source_target_pairs={{0,64},{64,0},{1,65},{65,1},{2,66},{66,2},{3,67},{67,3},{4,68},{68... | collective-permute-start | bytes 2162696 | tf_op jit(solution)/shard_map/ppermute | solution.py:329
  76.8 2.0 %grad_input.1 = bf16[1,4,16,64,128]{4,3,2,1,0:T(8,128)(2,1)} custom-call(bf16[1728,256]{1,0:T(8,128)(2,1)S(1)} %get-tuple-element.21.a_ref, bf16[3,384,256]{2,1,0:T(8,128)(2,1)S(1)} %get-tuple-element.22.r1_ref), custom_call_target="tpu_custom_call" | custom-call | flops 1200000000 | bytes 3000000 | tf_op jit(solution)/shard_map/grad_input/pallas_call | solution.py:294
  78.8 0.0 collective-permute-done.4.other_ref
  78.8 1.7 %output.1 = (f32[1728,128]{1,0:T(8,128)}, f32[3456,128]{1,0:T(8,128)}) custom-call(s32[1]{0:T(128)} %bitcast.core_ref, bf16[2816,128]{1,0:T(8,128)(2,1)S(1)} %bitcast.6, bf16[2816,128]{1,0:T(8,128)(2,1)S(1)} %collective-permute-done.4.other_ref), custom_call_target="tpu_custom_call" | custom-call | bytes 4000000 | tf_op jit(solution)/shard_map/output/pallas_call | solution.py:299
  (5 shorter events, 0.0 us)
Async XLA Ops:
  0.6 1.0 %copy-start = (bf16[1,2,8,64,128]{4,3,2,1,0:T(8,128)(2,1)S(1)}, bf16[1,2,8,64,128]{4,3,2,1,0:T(8,128)(2,1)}, u32[]{:S(2)}) copy-start(bf16[1,2,8,64,128]{4,3,2,1,0:T(8,128)(2,1)} %pre_ref.5) | copy-start | bytes 786436
  1.6 0.8 copy-start.5
  2.3 11.1 %copy-start.6 = (bf16[1,1,4,32,128]{4,3,2,1,0:T(8,128)(2,1)S(1)}, bf16[1,1,4,32,128]{4,3,2,1,0:T(8,128)(2,1)}, u32[]{:S(2)}) copy-start(bf16[1,1,4,32,128]{4,3,2,1,0:T(8,128)(2,1)} %og_ref.3) | copy-start | bytes 98308
  2.8 10.6 %collective-permute-start = (bf16[640,128]{1,0:T(8,128)(2,1)S(1)}, bf16[640,128]{1,0:T(8,128)(2,1)S(1)}, u32[]{:S(2)}, u32[]{:S(2)}) collective-permute-start(bf16[640,128]{1,0:T(8,128)(2,1)S(1)} %get-tuple-element.15), channel_id=1, source_target_pairs={{8,0},{16,8},{24,16},{32,24},{40,32},{48,40},{56,48},{9,1},{17,9},... | collective-permute-start | bytes 491528 | tf_op jit(solution)/shard_map/ppermute | solution.py:313
  4.1 9.3 %collective-permute-start.1 = (bf16[160,128]{1,0:T(8,128)(2,1)S(1)}, bf16[160,128]{1,0:T(8,128)(2,1)S(1)}, u32[]{:S(2)}, u32[]{:S(2)}) collective-permute-start(bf16[160,128]{1,0:T(8,128)(2,1)S(1)} %get-tuple-element.16), channel_id=1, source_target_pairs={{1,0},{2,1},{3,2},{4,3},{5,4},{6,5},{7,6},{9,8},{10,9},{11,10},{12... | collective-permute-start | bytes 122888 | tf_op jit(solution)/shard_map/ppermute | solution.py:315
  5.4 8.0 %collective-permute-start.2 = (bf16[96,128]{1,0:T(8,128)(2,1)S(1)}, bf16[96,128]{1,0:T(8,128)(2,1)S(1)}, u32[]{:S(2)}, u32[]{:S(2)}) collective-permute-start(bf16[96,128]{1,0:T(8,128)(2,1)S(1)} %get-tuple-element.17), channel_id=1, source_target_pairs={{9,0},{10,1},{11,2},{12,3},{13,4},{14,5},{15,6},{17,8},{18,9},{19,... | collective-permute-start | bytes 73736 | tf_op jit(solution)/shard_map/ppermute | solution.py:314
  6.7 1.0 %copy-start.1 = (bf16[1,2,8,64,128]{4,3,2,1,0:T(8,128)(2,1)S(1)}, bf16[1,2,8,64,128]{4,3,2,1,0:T(8,128)(2,1)}, u32[]{:S(2)}) copy-start(bf16[1,2,8,64,128]{4,3,2,1,0:T(8,128)(2,1)} %pre_ref.5) | copy-start | bytes 786436
  7.7 1.2 %copy-start.2 = (bf16[1,4,16,64,128]{4,3,2,1,0:T(8,128)(2,1)S(1)}, bf16[1,4,16,64,128]{4,3,2,1,0:T(8,128)(2,1)}, u32[]{:S(2)}) copy-start(bf16[1,4,16,64,128]{4,3,2,1,0:T(8,128)(2,1)} %u_ref.1) | copy-start | bytes 3145732
  8.9 1.2 %copy-start.3 = (bf16[3,3,3,128,128]{4,3,2,1,0:T(8,128)(2,1)S(1)}, bf16[3,3,3,128,128]{4,3,2,1,0:T(8,128)(2,1)}, u32[]{:S(2)}) copy-start(bf16[3,3,3,128,128]{4,3,2,1,0:T(8,128)(2,1)} %w2_ref.1) | copy-start | bytes 2654212
  10.1 1.0 %copy-start.4 = (bf16[3,3,3,64,128]{4,3,2,1,0:T(8,128)(2,1)S(1)}, bf16[3,3,3,64,128]{4,3,2,1,0:T(8,128)(2,1)}, u32[]{:S(2)}) copy-start(bf16[3,3,3,64,128]{4,3,2,1,0:T(8,128)(2,1)} %w1_ref.1) | copy-start | bytes 1327108
  15.3 5.5 %collective-permute-start.3 = (bf16[2816,128]{1,0:T(8,128)(2,1)S(1)}, bf16[2816,128]{1,0:T(8,128)(2,1)S(1)}, u32[]{:S(2)}, u32[]{:S(2)}) collective-permute-start(bf16[2816,128]{1,0:T(8,128)(2,1)S(1)} %get-tuple-element.24), channel_id=1, source_target_pairs={{0,64},{64,0},{1,65},{65,1},{2,66},{66,2},{3,67},{67,3},{4,68},{68... | collective-permute-start | bytes 2162696 | tf_op jit(solution)/shard_map/ppermute | solution.py:318
  73.1 5.6 %collective-permute-start.4 = (bf16[2816,128]{1,0:T(8,128)(2,1)S(1)}, bf16[2816,128]{1,0:T(8,128)(2,1)S(1)}, u32[]{:S(2)}, u32[]{:S(2)}) collective-permute-start(bf16[2816,128]{1,0:T(8,128)(2,1)S(1)} %bitcast.5), channel_id=1, source_target_pairs={{0,64},{64,0},{1,65},{65,1},{2,66},{66,2},{3,67},{67,3},{4,68},{68... | collective-permute-start | bytes 2162696 | tf_op jit(solution)/shard_map/ppermute | solution.py:329

commit v3 on v2

--- a/solution.py
+++ b/solution.py
@@ -64,7 +64,20 @@
         c.wait()
 
 
-def prep_kernel(u_ref, pre_ref, w1_ref, w2_ref, r1_ref, r2_ref, u1t_ref, u2t_ref, act_s):
+def prep_kernel(
+    u_hbm, pre_hbm, og_hbm, w1_hbm, w2_hbm,
+    r1_ref, r2_ref, u1t_ref, u2t_ref, pre_ref, og_ref,
+    u_ref, w1_ref, w2_ref, act_s, sems,
+):
+    w1_copy, w2_copy, pre_copy, u_copy, og_copy = [
+        pltpu.make_async_copy(source, target, sems.at[k])
+        for k, (source, target) in enumerate(
+            ((w1_hbm, w1_ref), (w2_hbm, w2_ref), (pre_hbm, pre_ref), (u_hbm, u_ref), (og_hbm, og_ref))
+        )
+    ]
+    for copy in (w1_copy, w2_copy, pre_copy, u_copy, og_copy):
+        copy.start()
+    w1_copy.wait()
     zero = jnp.zeros((CIN, C1), BF)
     for kx in range(3):
         for ky in range(3):
@@ -74,6 +87,7 @@
             r1_ref[kx, at + CIN : at + 2 * CIN, 0:C1] = w1_ref[kx, ky, 2]
             r1_ref[kx, at + CIN : at + 2 * CIN, C1:] = w1_ref[kx, ky, 0]
 
+    w2_copy.wait()
     zero = jnp.zeros((C1, C2), BF)
     for kx in range(3):
         for ky in range(3):
@@ -83,6 +97,7 @@
             r2_ref[t, C1:, 0:C2] = w2_ref[kx, ky, 2]
             r2_ref[t, C1:, C2:] = w2_ref[kx, ky, 0]
 
+    pre_copy.wait()
     own = MY * MZ
     for mx in range(MX):
         pre = pre_ref[0, mx].reshape(own, C1).astype(F32)
@@ -96,6 +111,7 @@
                 ]
                 u2t_ref[px * 2 + py, s * C1 : (s + 1) * C1, :] = jnp.concatenate(rows, 0).T.astype(BF)
 
+    u_copy.wait()
     for px in range(2):
         for py in range(2):
             for i in range(MX):
@@ -105,6 +121,7 @@
                     )
                     at = (i * MY + j) * MZ
                     u1t_ref[px * 2 + py, :, at : at + 2 * MZ] = pair.T
+    og_copy.wait()
 
 
 def main_kernel(
@@ -212,30 +229,44 @@
                     out_ref[0, 2 * i + px, 2 * (j + e) + 1] = odd[rows]
 
 
-def output_kernel(core_ref, mine_ref, other_ref, one_ref, two_ref):
+def output_kernel(second, core_ref, half_ref, *refs):
+    one_hbm, two_hbm, wide, sems = refs[-4:]
     low = HALF - ROWS_ONE
     high = ROWS_TWO - low
 
-    def put(first_ref, second_ref):
-        one_ref[...] = first_ref[0:ROWS_ONE].astype(F32)
-        two_ref[0:low] = first_ref[ROWS_ONE:].astype(F32)
-        two_ref[low:] = second_ref[0:high].astype(F32)
-
-    @pl.when(core_ref[0] == 0)
+    def put(parts):
+        copies = []
+        for k, (at, rows, target, to) in enumerate(parts):
+            wide[at : at + rows] = half_ref[at : at + rows].astype(F32)
+            copies.append(
+                pltpu.make_async_copy(
+                    wide.at[pl.ds(at, rows)], target.at[pl.ds(to, rows)], sems.at[k]
+                )
+            )
+            copies[-1].start()
+        for copy in copies:
+            copy.wait()
+
+    @pl.when(core_ref[0] == second)
     def _():
-        put(mine_ref, other_ref)
-
-    @pl.when(core_ref[0] != 0)
+        put(((0, ROWS_ONE // 2, one_hbm, 0), (ROWS_ONE // 2, ROWS_ONE // 2, one_hbm, ROWS_ONE // 2), (ROWS_ONE, low, two_hbm, 0)))
+
+    @pl.when(core_ref[0] != second)
     def _():
-        put(other_ref, mine_ref)
+        third = 792
+        put(((0, third, two_hbm, low), (third, third, two_hbm, low + third), (2 * third, high - 2 * third, two_hbm, low + 2 * third)))
 
 
 def vmem(n):
     return [pl.BlockSpec(memory_space=pltpu.VMEM)] * n
 
 
-def near(x):
-    return pltpu.with_memory_space_constraint(x, pltpu.VMEM)
+def hbm(n):
+    return [pl.BlockSpec(memory_space=pltpu.HBM)] * n
+
+
+def far(*arrays):
+    return [pltpu.with_memory_space_constraint(x, pltpu.HBM) for x in arrays]
 
 
 SMEM = pl.BlockSpec(memory_space=pltpu.SMEM)
@@ -258,19 +289,26 @@
 def pack_call(pre, og):
     out = [pltpu.VMEM(((CY * CZ + MY * MZ), C1), BF), pltpu.VMEM((CZ + MX * MZ, C1), BF), pltpu.VMEM((CZ + MZ, C1), BF)]
     count = CY + MY + 1 + MX + 2
-    any_spec = [pl.BlockSpec(memory_space=pl.ANY)] * 2
-    return call(pack_kernel, "pack", out, [pltpu.SemaphoreType.DMA((count,))], any_spec, 0, 500_000)(pre, og)
-
-
-def prep_call(u, pre, w1, w2):
+    return call(pack_kernel, "pack", out, [pltpu.SemaphoreType.DMA((count,))], hbm(2), 0, 500_000)(*far(pre, og))
+
+
+def prep_call(u, pre, og, w1, w2):
     out = [
         pltpu.VMEM((3, 6 * CIN, 2 * C1), BF),
         pltpu.VMEM((9, 2 * C1, 2 * C2), BF),
         pltpu.VMEM((4, 2 * CIN, MX * MY * MZ), BF),
         pltpu.VMEM((4, 2 * C1, CY * CZ), BF),
-    ]
-    scratch = [pltpu.VMEM((MX * MY * MZ, C1), F32)]
-    return call(prep_kernel, "prep", out, scratch, vmem(4), 0, 6_000_000)(u, pre, w1, w2)
+        pltpu.VMEM(pre.shape, BF),
+        pltpu.VMEM(og.shape, BF),
+    ]
+    scratch = [
+        pltpu.VMEM(u.shape, BF),
+        pltpu.VMEM(w1.shape, BF),
+        pltpu.VMEM(w2.shape, BF),
+        pltpu.VMEM((MX * MY * MZ, C1), F32),
+        pltpu.SemaphoreType.DMA((5,)),
+    ]
+    return call(prep_kernel, "prep", out, scratch, hbm(5), 0, 6_000_000)(*far(u, pre, og, w1, w2))
 
 
 def main_call(core, pre, og, hx, hy, hc, r2, u1t, u2t):
@@ -294,9 +332,22 @@
     return call(input_kernel, "grad_input", out, [], vmem(2), 1_200_000_000, 3_000_000)(a, r1)[0]
 
 
-def output_call(core, mine, other):
-    out = [jax.ShapeDtypeStruct((ROWS_ONE, C1), F32), jax.ShapeDtypeStruct((ROWS_TWO, C1), F32)]
-    return call(output_kernel, "output", out, [], [SMEM] + vmem(2), 0, 4_000_000)(core, mine, other)
+def output_call(core, half, before=()):
+    second = len(before) // 2
+    return pl.pallas_call(
+        functools.partial(output_kernel, second),
+        out_shape=(
+            jax.ShapeDtypeStruct((ROWS_ONE, C1), F32),
+            jax.ShapeDtypeStruct((ROWS_TWO, C1), F32),
+        ),
+        in_specs=[SMEM] + vmem(1) + hbm(len(before)),
+        out_specs=tuple(hbm(2)),
+        scratch_shapes=[pltpu.VMEM((HALF, C1), F32), pltpu.SemaphoreType.DMA((3,))],
+        input_output_aliases={2: 0, 3: 1} if second else {},
+        cost_estimate=pl.CostEstimate(flops=0, bytes_accessed=2_000_000, transcendentals=0),
+        compiler_params=pltpu.CompilerParams(vmem_limit_bytes=LIMIT),
+        name="output",
+    )(core, half, *before)
 
 
 def on_device(u, pre, og, w1, w2):
@@ -313,10 +364,11 @@
     hx = lax.ppermute(hx, AX, from_x)
     hc = lax.ppermute(hc, AX + AZ, from_xz)
     hy = lax.ppermute(hy, AZ, from_z)
-    r1, r2, u1t, u2t = prep_call(u, pre, w1, w2)
+    r1, r2, u1t, u2t, pre, og = prep_call(u, pre, og, w1, w2)
     a, keep, send = main_call(core, pre, og, hx, hy, hc, r2, u1t, u2t)
     received = lax.ppermute(send, "core", [(0, 1), (1, 0)])
     grad_input = input_call(a, r1)
+    received, grad_input = lax.optimization_barrier((received, grad_input))
 
     group = ("xh", "y", "xl", "zl")
     half = (keep.astype(F32) + received.astype(F32)).astype(BF).reshape(GROUP, CHUNK, C1)
@@ -327,7 +379,7 @@
     mine = lax.all_to_all(jnp.broadcast_to(chunk[None], (GROUP, CHUNK, C1)), group, 0, 0, tiled=True)
     mine = mine.reshape(HALF, C1)
     other = lax.ppermute(mine, "core", [(0, 1), (1, 0)])
-    grad_one, grad_two = output_call(core, mine, other)
+    grad_one, grad_two = output_call(core, other, output_call(core, mine))
     return grad_input, grad_one.reshape(3, 3, 3, CIN, C1), grad_two.reshape(3, 3, 3, C1, C2)
 
 

time: 81 us -> 78.7 us (0.972)
  local copies, waits for them, and re-layouts: 6.16 us -> 0.11 us
  Pallas kernels: 6.62 us -> 9.13 us
  waiting for transfers between devices: 3.48 us -> 5.35 us
    unnamed x14 -> x0, local copies, waits for them, and re-layouts: 6.06 us -> none
    ppermute x1, waiting for transfers between devices: 1.65 us -> 4.6 us  [on_device(): hc = lax.ppermute(hc, AX + AZ, from_xz)]
    pallas_call x3 -> x4, Pallas kernels: 2.81 us -> 5.36 us  [the longest x2 2.22 us: output_call(): pl.pallas_call(functools.partial(output_kernel, second), out_shape=(jax.S...]
    ppermute x1, waiting for transfers between devices: 1.82 us -> 0.01 us  [on_device(): received = lax.ppermute(send, 'core', [(0, 1), (1, 0)])]
  transfers between devices with their start and end apart: 5 -> 5, of which waited for: 2 -> 2; matrix products, arithmetic and copies ran while one was open for 0% -> 0% of each run, Pallas kernels for 3% -> 7%
where the time goes in v3:
time: 78.7 us; the launch traced here: 78.3 us
  blocking collectives  51.5 us (65%)
  starting transfers between devices  11.2 us (14%)
  Pallas kernels  9.13 us (12%)
  waiting for transfers between devices  5.35 us (7%)
    all_to_all x1, blocking collectives, on_device(): parts = lax.all_to_all(half, group, 0, 0, tiled=True)  21.4 us
    all_to_all x1, blocking collectives, on_device(): lax.all_to_all(jnp.broadcast_to(chunk[None], (GROUP, CHUNK, C1)), group,...  15.1 us
    all_to_all x1, blocking collectives, on_device(): lax.all_to_all(jnp.broadcast_to(chunk[None], (4, CHUNK, C1)), 'zh', 0, 0,...  15 us
    ppermute x1, waiting for transfers between devices, on_device(): hc = lax.ppermute(hc, AX + AZ, from_xz)  4.6 us
    ppermute x1, starting transfers between devices, on_device(): received = lax.ppermute(send, 'core', [(0, 1), (1, 0)])  3.71 us
    ppermute x1, starting transfers between devices, on_device(): other = lax.ppermute(mine, 'core', [(0, 1), (1, 0)])  3.58 us
    pallas_call x2, Pallas kernels, output_call(): pl.pallas_call(functools.partial(output_kernel, second), out_shape=(jax.S...  2.22 us
    pallas_call x1, Pallas kernels, prep_call(): call(prep_kernel, 'prep', out, scratch, hbm(5), 0, 6000000)  2.08 us
  transfers between devices with their start and end apart: 5, of which 2 were waited for; matrix products, arithmetic and copies ran while one was open for 0% of the time, Pallas kernels for 7%

profile of v3, /device:TPU:1, one launch (start us, length us, event | category | flops | bytes accessed | tf_op | source)
XLA Modules:
  0.0 78.3 jit_solution(12870145014594562479)
XLA Ops:
  0.6 1.1 %pack.1 = (bf16[640,128]{1,0:T(8,128)(2,1)S(1)}, bf16[160,128]{1,0:T(8,128)(2,1)S(1)}, bf16[96,128]{1,0:T(8,128)(2,1)S(1)}) custom-call(bf16[1,2,8,64,128]{4,3,2,1,0:T(8,128)(2,1)} %pre_ref.1, bf16[1,1,4,32,128]{4,3,2,1,0:T(8,128)(2,1)} %og_ref.1), custom_call_target="tpu_custom_call" | custom-call | bytes 500000 | tf_op jit(solution)/shard_map/pack/pallas_call | solution.py:292
  1.7 1.3 %collective-permute-start = (bf16[640,128]{1,0:T(8,128)(2,1)S(1)}, bf16[640,128]{1,0:T(8,128)(2,1)S(1)}, u32[]{:S(2)}, u32[]{:S(2)}) collective-permute-start(bf16[640,128]{1,0:T(8,128)(2,1)S(1)} %get-tuple-element.23), channel_id=1, source_target_pairs={{8,0},{16,8},{24,16},{32,24},{40,32},{48,40},{56,48},{9,1},{17,9},... | collective-permute-start | bytes 491528 | tf_op jit(solution)/shard_map/ppermute | solution.py:364
  3.0 1.3 %collective-permute-start.1 = (bf16[160,128]{1,0:T(8,128)(2,1)S(1)}, bf16[160,128]{1,0:T(8,128)(2,1)S(1)}, u32[]{:S(2)}, u32[]{:S(2)}) collective-permute-start(bf16[160,128]{1,0:T(8,128)(2,1)S(1)} %get-tuple-element.24), channel_id=1, source_target_pairs={{1,0},{2,1},{3,2},{4,3},{5,4},{6,5},{7,6},{9,8},{10,9},{11,10},{12... | collective-permute-start | bytes 122888 | tf_op jit(solution)/shard_map/ppermute | solution.py:366
  4.3 1.3 %collective-permute-start.2 = (bf16[96,128]{1,0:T(8,128)(2,1)S(1)}, bf16[96,128]{1,0:T(8,128)(2,1)S(1)}, u32[]{:S(2)}, u32[]{:S(2)}) collective-permute-start(bf16[96,128]{1,0:T(8,128)(2,1)S(1)} %get-tuple-element.25), channel_id=1, source_target_pairs={{9,0},{10,1},{11,2},{12,3},{13,4},{14,5},{15,6},{17,8},{18,9},{19,... | collective-permute-start | bytes 73736 | tf_op jit(solution)/shard_map/ppermute | solution.py:365
  5.6 2.1 %prep.1 = (bf16[3,384,256]{2,1,0:T(8,128)(2,1)S(1)}, bf16[9,256,256]{2,1,0:T(8,128)(2,1)S(1)}, bf16[4,128,1024]{2,1,0:T(8,128)(2,1)S(1)}, bf16[4,256,128]{2,1,0:...) custom-call(bf16[1,4,16,64,128]{4,3,2,1,0:T(8,128)(2,1)} %u_hbm.1, ...), custom_call_target="tpu_custom_call" | custom-call | bytes 6000000 | tf_op jit(solution)/shard_map/prep/pallas_call | solution.py:311
  7.7 4.6 %collective-permute-done.2.hc_ref = bf16[96,128]{1,0:T(8,128)(2,1)S(1)} collective-permute-done((bf16[96,128]{1,0:T(8,128)(2,1)S(1)}, bf16[96,128]{1,0:T(8,128)(2,1)S(1)}, u32[]{:S(2)}, u32[]{:S(2)}) %collective-permute-start.2) | collective-permute-done | bytes 24608 | tf_op jit(solution)/shard_map/ppermute | solution.py:365
  12.3 0.0 collective-permute-done.1.hy_ref
  12.3 0.0 collective-permute-done.hx_ref
  12.3 1.8 %main.1 = (bf16[1728,256]{1,0:T(8,128)(2,1)S(1)}, bf16[2816,128]{1,0:T(8,128)(2,1)S(1)}, bf16[2816,128]{1,0:T(8,128)(2,1)S(1)}) custom-call(s32[1]{0:T(128)} %bitcast.core_ref, bf16[1,2,8,64,128]{4,3,2,1,0:T(8,128)(2,1)S(1)} %get-tuple-element.21.pre_ref, bf16[1,1,4,32,128]{4,3,2,1,0:T(8,128)(2,1)S(1)} %get-tuple-element.22.og_ref, ...), custom_call_target="tpu_custom_call" | custom-call | flops 2000000000 | bytes 8000000 | tf_op jit(solution)/shard_map/main/pallas_call | solution.py:325
  14.1 3.7 %collective-permute-start.3 = (bf16[2816,128]{1,0:T(8,128)(2,1)S(1)}, bf16[2816,128]{1,0:T(8,128)(2,1)S(1)}, u32[]{:S(2)}, u32[]{:S(2)}) collective-permute-start(bf16[2816,128]{1,0:T(8,128)(2,1)S(1)} %get-tuple-element.29), channel_id=1, source_target_pairs={{0,64},{64,0},{1,65},{65,1},{2,66},{66,2},{3,67},{67,3},{4,68},{68... | collective-permute-start | bytes 2162696 | tf_op jit(solution)/shard_map/ppermute | solution.py:369
  17.8 2.0 %grad_input.1 = bf16[1,4,16,64,128]{4,3,2,1,0:T(8,128)(2,1)} custom-call(bf16[1728,256]{1,0:T(8,128)(2,1)S(1)} %get-tuple-element.30.a_ref, bf16[3,384,256]{2,1,0:T(8,128)(2,1)S(1)} %get-tuple-element.31.r1_ref), custom_call_target="tpu_custom_call" | custom-call | flops 1200000000 | bytes 3000000 | tf_op jit(solution)/shard_map/grad_input/pallas_call | solution.py:332
  19.8 0.0 collective-permute-done.3
  19.8 0.2 add_convert_fusion
  20.0 21.4 %all_to_all.15 = bf16[32,88,128]{2,1,0:T(8,128)(2,1)S(1)} all-to-all(bf16[32,88,128]{2,1,0:T(8,128)(2,1)S(1)} %bitcast.7), channel_id=1, replica_groups=mesh['xh'=2,'core'=2,'y'=4,'xl'=2,'zh'=4,'zl'=2] {'xh','y','xl','zl'}, dimensions={0} | all-to-all | bytes 1441792 | tf_op jit(solution)/shard_map/all_to_all | solution.py:375
  41.4 0.1 reduce_sum.24
  41.5 15.0 %all_to_all.16 = bf16[4,88,128]{2,1,0:T(8,128)(2,1)S(1)} all-to-all(bf16[4,88,128]{2,1,0:T(8,128)(2,1)S(1)} %broadcast_in_dim.4), channel_id=1, replica_groups=mesh['xh'=2,'core'=2,'y'=4,'xl'=2,'zh'=4,'zl'=2] {'zh'}, dimensions={0} | all-to-all | bytes 180224 | tf_op jit(solution)/shard_map/all_to_all | solution.py:377
  56.6 0.1 broadcast_in_dim.5
  56.7 15.1 %all_to_all.17 = bf16[32,88,128]{2,1,0:T(8,128)(2,1)S(1)} all-to-all(bf16[32,88,128]{2,1,0:T(8,128)(2,1)S(1)} %broadcast_in_dim.5), channel_id=1, replica_groups=mesh['xh'=2,'core'=2,'y'=4,'xl'=2,'zh'=4,'zl'=2] {'xh','y','xl','zl'}, dimensions={0} | all-to-all | bytes 1441792 | tf_op jit(solution)/shard_map/all_to_all | solution.py:379
  71.8 3.6 %collective-permute-start.4 = (bf16[2816,128]{1,0:T(8,128)(2,1)S(1)}, bf16[2816,128]{1,0:T(8,128)(2,1)S(1)}, u32[]{:S(2)}, u32[]{:S(2)}) collective-permute-start(bf16[2816,128]{1,0:T(8,128)(2,1)S(1)} %bitcast.5), channel_id=1, source_target_pairs={{0,64},{64,0},{1,65},{65,1},{2,66},{66,2},{3,67},{67,3},{4,68},{68... | collective-permute-start | bytes 2162696 | tf_op jit(solution)/shard_map/ppermute | solution.py:381
  75.4 1.1 %output.2 = (f32[1728,128]{1,0:T(8,128)}, f32[3456,128]{1,0:T(8,128)}) custom-call(s32[1]{0:T(128)} %bitcast.core_ref, bf16[2816,128]{1,0:T(8,128)(2,1)S(1)} %bitcast.6), custom_call_target="tpu_custom_call" | custom-call | bytes 2000000 | tf_op jit(solution)/shard_map/output/pallas_call | solution.py:337
  76.4 0.7 collective-permute-done.4.half_ref
  77.2 1.1 %output.3 = (f32[1728,128]{1,0:T(8,128)}, f32[3456,128]{1,0:T(8,128)}) custom-call(s32[1]{0:T(128)} %bitcast.core_ref, bf16[2816,128]{1,0:T(8,128)(2,1)S(1)} %collective-permute-done.4.half_ref, f32[1728,128]{1,0:T(8,128)} %get-tuple-element.35.refs_0_, f32[3456,128]{1,0:T(8,128)} %get-tuple-element.36.refs_1_), custom_call_target="tpu_custom_call", output_to_operand_aliasing={{0}: (2, {}), {1}: (3, {})} | custom-call | bytes 2000000 | tf_op jit(solution)/shard_map/output/pallas_call | solution.py:337
  (2 shorter events, 0.0 us)
Async XLA Ops:
  1.7 10.6 %collective-permute-start = (bf16[640,128]{1,0:T(8,128)(2,1)S(1)}, bf16[640,128]{1,0:T(8,128)(2,1)S(1)}, u32[]{:S(2)}, u32[]{:S(2)}) collective-permute-start(bf16[640,128]{1,0:T(8,128)(2,1)S(1)} %get-tuple-element.23), channel_id=1, source_target_pairs={{8,0},{16,8},{24,16},{32,24},{40,32},{48,40},{56,48},{9,1},{17,9},... | collective-permute-start | bytes 491528 | tf_op jit(solution)/shard_map/ppermute | solution.py:364
  3.0 9.3 %collective-permute-start.1 = (bf16[160,128]{1,0:T(8,128)(2,1)S(1)}, bf16[160,128]{1,0:T(8,128)(2,1)S(1)}, u32[]{:S(2)}, u32[]{:S(2)}) collective-permute-start(bf16[160,128]{1,0:T(8,128)(2,1)S(1)} %get-tuple-element.24), channel_id=1, source_target_pairs={{1,0},{2,1},{3,2},{4,3},{5,4},{6,5},{7,6},{9,8},{10,9},{11,10},{12... | collective-permute-start | bytes 122888 | tf_op jit(solution)/shard_map/ppermute | solution.py:366
  4.3 8.0 %collective-permute-start.2 = (bf16[96,128]{1,0:T(8,128)(2,1)S(1)}, bf16[96,128]{1,0:T(8,128)(2,1)S(1)}, u32[]{:S(2)}, u32[]{:S(2)}) collective-permute-start(bf16[96,128]{1,0:T(8,128)(2,1)S(1)} %get-tuple-element.25), channel_id=1, source_target_pairs={{9,0},{10,1},{11,2},{12,3},{13,4},{14,5},{15,6},{17,8},{18,9},{19,... | collective-permute-start | bytes 73736 | tf_op jit(solution)/shard_map/ppermute | solution.py:365
  14.1 5.7 %collective-permute-start.3 = (bf16[2816,128]{1,0:T(8,128)(2,1)S(1)}, bf16[2816,128]{1,0:T(8,128)(2,1)S(1)}, u32[]{:S(2)}, u32[]{:S(2)}) collective-permute-start(bf16[2816,128]{1,0:T(8,128)(2,1)S(1)} %get-tuple-element.29), channel_id=1, source_target_pairs={{0,64},{64,0},{1,65},{65,1},{2,66},{66,2},{3,67},{67,3},{4,68},{68... | collective-permute-start | bytes 2162696 | tf_op jit(solution)/shard_map/ppermute | solution.py:369
  71.8 5.4 %collective-permute-start.4 = (bf16[2816,128]{1,0:T(8,128)(2,1)S(1)}, bf16[2816,128]{1,0:T(8,128)(2,1)S(1)}, u32[]{:S(2)}, u32[]{:S(2)}) collective-permute-start(bf16[2816,128]{1,0:T(8,128)(2,1)S(1)} %bitcast.5), channel_id=1, source_target_pairs={{0,64},{64,0},{1,65},{65,1},{2,66},{66,2},{3,67},{67,3},{4,68},{68... | collective-permute-start | bytes 2162696 | tf_op jit(solution)/shard_map/ppermute | solution.py:381

commit v4 on v3

--- a/solution.py
+++ b/solution.py
@@ -16,6 +16,8 @@
 CIN, C1, C2 = 64, 128, 128
 EX, EY = MX + 1, MY + 1
 CHUNK = 88
+AX = ("y", "xl")
+AZ = ("zh", "zl")
 GROUP = 32
 HALF = CHUNK * GROUP
 ROWS_ONE = 27 * CIN
@@ -125,7 +127,7 @@
 
 
 def main_kernel(
-    core_ref, pre_ref, og_ref, hx_ref, hy_ref, hc_ref, r2_ref, u1t_ref, u2t_ref,
+    pre_ref, og_ref, hx_ref, hy_ref, hc_ref, r2_ref, u1t_ref, u2t_ref,
     a_ref, keep_ref, send_ref,
     b_s, ga_s, buf_s,
 ):
@@ -134,10 +136,15 @@
         b_s[at : at + n, 0:C2] = value
         b_s[at : at + n, C2:] = next_row(value.astype(F32), CZ).astype(BF)
 
+    def inside(value, edge):
+        return jnp.where(edge > 0, 0.0, value.astype(F32)).astype(BF)
+
+    edge_x = (lax.axis_index(AX) == lax.axis_size(AX) - 1).astype(jnp.int32)
+    edge_y = (lax.axis_index(AZ) == lax.axis_size(AZ) - 1).astype(jnp.int32)
     put_b(0, og_ref[0, 0].reshape(CY * CZ, C2))
-    put_b(CY * CZ, hy_ref[0:CZ])
-    put_b((CY + 1) * CZ, hx_ref[0 : CY * CZ])
-    put_b((2 * CY + 1) * CZ, hc_ref[0:CZ])
+    put_b(CY * CZ, inside(hy_ref[0:CZ], edge_y))
+    put_b((CY + 1) * CZ, inside(hx_ref[0 : CY * CZ], edge_x))
+    put_b((2 * CY + 1) * CZ, inside(hc_ref[0:CZ], edge_x + edge_y))
 
     def put_ga(mx, my, value):
         base = (mx * EY + my) * MZ
@@ -202,7 +209,7 @@
             buf_s[at + CIN : at + 2 * CIN, :] = d[0:CIN, 0:C1].astype(BF)
             buf_s[at + 2 * CIN : at + 3 * CIN, :] = d[CIN:, 0:C1].astype(BF)
 
-    core = core_ref[0]
+    core = lax.axis_index("core")
     keep_ref[...] = buf_s[pl.ds(pl.multiple_of(core * HALF, HALF), HALF), :]
     send_ref[...] = buf_s[pl.ds(pl.multiple_of((1 - core) * HALF, HALF), HALF), :]
 
@@ -229,7 +236,7 @@
                     out_ref[0, 2 * i + px, 2 * (j + e) + 1] = odd[rows]
 
 
-def output_kernel(second, core_ref, half_ref, *refs):
+def output_kernel(second, half_ref, *refs):
     one_hbm, two_hbm, wide, sems = refs[-4:]
     low = HALF - ROWS_ONE
     high = ROWS_TWO - low
@@ -247,11 +254,11 @@
         for copy in copies:
             copy.wait()
 
-    @pl.when(core_ref[0] == second)
+    @pl.when(lax.axis_index("core") == second)
     def _():
         put(((0, ROWS_ONE // 2, one_hbm, 0), (ROWS_ONE // 2, ROWS_ONE // 2, one_hbm, ROWS_ONE // 2), (ROWS_ONE, low, two_hbm, 0)))
 
-    @pl.when(core_ref[0] != second)
+    @pl.when(lax.axis_index("core") != second)
     def _():
         third = 792
         put(((0, third, two_hbm, low), (third, third, two_hbm, low + third), (2 * third, high - 2 * third, two_hbm, low + 2 * third)))
@@ -269,7 +276,6 @@
     return [pltpu.with_memory_space_constraint(x, pltpu.HBM) for x in arrays]
 
 
-SMEM = pl.BlockSpec(memory_space=pltpu.SMEM)
 LIMIT = 20 * 1024 * 1024
 
 
@@ -311,7 +317,7 @@
     return call(prep_kernel, "prep", out, scratch, hbm(5), 0, 6_000_000)(*far(u, pre, og, w1, w2))
 
 
-def main_call(core, pre, og, hx, hy, hc, r2, u1t, u2t):
+def main_call(pre, og, hx, hy, hc, r2, u1t, u2t):
     out = [
         pltpu.VMEM((EX * EY * MZ, 2 * C1), BF),
         pltpu.VMEM((HALF, C1), BF),
@@ -322,8 +328,8 @@
         pltpu.VMEM((EX * EY * MZ, C1), F32),
         pltpu.VMEM((ROWS, C1), BF),
     ]
-    return call(main_kernel, "main", out, scratch, [SMEM] + vmem(8), 2_000_000_000, 8_000_000)(
-        core, pre, og, hx, hy, hc, r2, u1t, u2t
+    return call(main_kernel, "main", out, scratch, vmem(8), 2_000_000_000, 8_000_000)(
+        pre, og, hx, hy, hc, r2, u1t, u2t
     )
 
 
@@ -332,7 +338,7 @@
     return call(input_kernel, "grad_input", out, [], vmem(2), 1_200_000_000, 3_000_000)(a, r1)[0]
 
 
-def output_call(core, half, before=()):
+def output_call(half, before=()):
     second = len(before) // 2
     return pl.pallas_call(
         functools.partial(output_kernel, second),
@@ -340,32 +346,30 @@
             jax.ShapeDtypeStruct((ROWS_ONE, C1), F32),
             jax.ShapeDtypeStruct((ROWS_TWO, C1), F32),
         ),
-        in_specs=[SMEM] + vmem(1) + hbm(len(before)),
+        in_specs=vmem(1) + hbm(len(before)),
         out_specs=tuple(hbm(2)),
         scratch_shapes=[pltpu.VMEM((HALF, C1), F32), pltpu.SemaphoreType.DMA((3,))],
-        input_output_aliases={2: 0, 3: 1} if second else {},
+        input_output_aliases={1: 0, 2: 1} if second else {},
         cost_estimate=pl.CostEstimate(flops=0, bytes_accessed=2_000_000, transcendentals=0),
         compiler_params=pltpu.CompilerParams(vmem_limit_bytes=LIMIT),
         name="output",
-    )(core, half, *before)
+    )(half, *before)
 
 
 def on_device(u, pre, og, w1, w2):
-    core = lax.axis_index("core").reshape(1)
     sx = lax.axis_size("y") * lax.axis_size("xl")
     sz = lax.axis_size("zh") * lax.axis_size("zl")
-    AX, AZ = ("y", "xl"), ("zh", "zl")
-    from_x = [(i + 1, i) for i in range(sx - 1)]
-    from_z = [(i + 1, i) for i in range(sz - 1)]
+    from_x = [((i + 1) % sx, i) for i in range(sx)]
+    from_z = [((i + 1) % sz, i) for i in range(sz)]
     from_xz = [
-        ((i + 1) * sz + j + 1, i * sz + j) for i in range(sx - 1) for j in range(sz - 1)
+        ((i + 1) % sx * sz + (j + 1) % sz, i * sz + j) for i in range(sx) for j in range(sz)
     ]
     hx, hy, hc = pack_call(pre, og)
     hx = lax.ppermute(hx, AX, from_x)
     hc = lax.ppermute(hc, AX + AZ, from_xz)
     hy = lax.ppermute(hy, AZ, from_z)
     r1, r2, u1t, u2t, pre, og = prep_call(u, pre, og, w1, w2)
-    a, keep, send = main_call(core, pre, og, hx, hy, hc, r2, u1t, u2t)
+    a, keep, send = main_call(pre, og, hx, hy, hc, r2, u1t, u2t)
     received = lax.ppermute(send, "core", [(0, 1), (1, 0)])
     grad_input = input_call(a, r1)
     received, grad_input = lax.optimization_barrier((received, grad_input))
@@ -379,7 +383,7 @@
     mine = lax.all_to_all(jnp.broadcast_to(chunk[None], (GROUP, CHUNK, C1)), group, 0, 0, tiled=True)
     mine = mine.reshape(HALF, C1)
     other = lax.ppermute(mine, "core", [(0, 1), (1, 0)])
-    grad_one, grad_two = output_call(core, other, output_call(core, mine))
+    grad_one, grad_two = output_call(other, output_call(mine))
     return grad_input, grad_one.reshape(3, 3, 3, CIN, C1), grad_two.reshape(3, 3, 3, C1, C2)
 
 

time: 78.7 us -> 74.4 us (0.945)
  blocking collectives: 51.5 us -> 45.4 us
  starting transfers between devices: 11.2 us -> 16.9 us
  waiting for transfers between devices: 5.35 us -> 1.54 us
    ppermute x1, starting transfers between devices: 1.29 us -> 5.58 us  [on_device(): hy = lax.ppermute(hy, AZ, from_z)]
    all_to_all x1, blocking collectives: 15 us -> 10.9 us  [on_device(): lax.all_to_all(jnp.broadcast_to(chunk[None], (4, CHUNK, C1)), 'zh', 0, 0,...]
    ppermute x1, waiting for transfers between devices: 4.6 us -> 0.79 us  [on_device(): hc = lax.ppermute(hc, AX + AZ, from_xz)]
    ppermute x1, starting transfers between devices: 1.29 us -> 4.56 us  [on_device(): hx = lax.ppermute(hx, AX, from_x)]
    all_to_all x1, blocking collectives: 21.4 us -> 19.3 us  [on_device(): parts = lax.all_to_all(half, group, 0, 0, tiled=True)]
    ppermute x1, starting transfers between devices: 3.71 us -> 2.49 us  [on_device(): received = lax.ppermute(send, 'core', [(0, 1), (1, 0)])]
where the time goes in v4:
time: 74.4 us; the launch traced here: 74 us
  blocking collectives  45.4 us (61%)
  starting transfers between devices  16.9 us (23%)
  Pallas kernels  9.11 us (12%)
  waiting for transfers between devices  1.54 us (2%)
    all_to_all x1, blocking collectives, on_device(): parts = lax.all_to_all(half, group, 0, 0, tiled=True)  19.3 us
    all_to_all x1, blocking collectives, on_device(): lax.all_to_all(jnp.broadcast_to(chunk[None], (GROUP, CHUNK, C1)), group,...  15.1 us
    all_to_all x1, blocking collectives, on_device(): lax.all_to_all(jnp.broadcast_to(chunk[None], (4, CHUNK, C1)), 'zh', 0, 0,...  10.9 us
    ppermute x1, starting transfers between devices, on_device(): hy = lax.ppermute(hy, AZ, from_z)  5.58 us
    ppermute x1, starting transfers between devices, on_device(): hx = lax.ppermute(hx, AX, from_x)  4.56 us
    ppermute x1, starting transfers between devices, on_device(): other = lax.ppermute(mine, 'core', [(0, 1), (1, 0)])  3.58 us
    ppermute x1, starting transfers between devices, on_device(): received = lax.ppermute(send, 'core', [(0, 1), (1, 0)])  2.49 us
    pallas_call x2, Pallas kernels, output_call(): pl.pallas_call(functools.partial(output_kernel, second), out_shape=(jax.S...  2.22 us
  transfers between devices with their start and end apart: 5, of which 2 were waited for; matrix products, arithmetic and copies ran while one was open for 0% of the time, Pallas kernels for 7%

profile of v4, /device:TPU:1, one launch (start us, length us, event | category | flops | bytes accessed | tf_op | source)
XLA Modules:
  0.0 74.0 jit_solution(1966527397416740256)
XLA Ops:
  0.6 1.1 %pack.1 = (bf16[640,128]{1,0:T(8,128)(2,1)S(1)}, bf16[160,128]{1,0:T(8,128)(2,1)S(1)}, bf16[96,128]{1,0:T(8,128)(2,1)S(1)}) custom-call(bf16[1,2,8,64,128]{4,3,2,1,0:T(8,128)(2,1)} %pre_ref.1, bf16[1,1,4,32,128]{4,3,2,1,0:T(8,128)(2,1)} %og_ref.1), custom_call_target="tpu_custom_call" | custom-call | bytes 500000 | tf_op jit(solution)/shard_map/pack/pallas_call | solution.py:298
  1.7 4.6 %collective-permute-start = (bf16[640,128]{1,0:T(8,128)(2,1)S(1)}, bf16[640,128]{1,0:T(8,128)(2,1)S(1)}, u32[]{:S(2)}, u32[]{:S(2)}) collective-permute-start(bf16[640,128]{1,0:T(8,128)(2,1)S(1)} %get-tuple-element.23), channel_id=1, source_target_pairs={{8,0},{16,8},{24,16},{32,24},{40,32},{48,40},{56,48},{0,56},{9,1},... | collective-permute-start | bytes 491528 | tf_op jit(solution)/shard_map/ppermute | solution.py:368
  6.3 5.6 %collective-permute-start.1 = (bf16[160,128]{1,0:T(8,128)(2,1)S(1)}, bf16[160,128]{1,0:T(8,128)(2,1)S(1)}, u32[]{:S(2)}, u32[]{:S(2)}) collective-permute-start(bf16[160,128]{1,0:T(8,128)(2,1)S(1)} %get-tuple-element.24), channel_id=1, source_target_pairs={{1,0},{2,1},{3,2},{4,3},{5,4},{6,5},{7,6},{0,7},{9,8},{10,9},{11,1... | collective-permute-start | bytes 122888 | tf_op jit(solution)/shard_map/ppermute | solution.py:370
  11.8 0.7 collective-permute-start.2
  12.5 2.1 %prep.1 = (bf16[3,384,256]{2,1,0:T(8,128)(2,1)S(1)}, bf16[9,256,256]{2,1,0:T(8,128)(2,1)S(1)}, bf16[4,128,1024]{2,1,0:T(8,128)(2,1)S(1)}, bf16[4,256,128]{2,1,0:...) custom-call(bf16[1,4,16,64,128]{4,3,2,1,0:T(8,128)(2,1)} %u_hbm.1, ...), custom_call_target="tpu_custom_call" | custom-call | bytes 6000000 | tf_op jit(solution)/shard_map/prep/pallas_call | solution.py:317
  14.6 0.8 %collective-permute-done.2.hc_ref = bf16[96,128]{1,0:T(8,128)(2,1)S(1)} collective-permute-done((bf16[96,128]{1,0:T(8,128)(2,1)S(1)}, bf16[96,128]{1,0:T(8,128)(2,1)S(1)}, u32[]{:S(2)}, u32[]{:S(2)}) %collective-permute-start.2) | collective-permute-done | bytes 24608 | tf_op jit(solution)/shard_map/ppermute | solution.py:369
  15.4 0.0 collective-permute-done.1.hy_ref
  15.4 0.0 collective-permute-done.hx_ref
  15.4 1.8 %main.1 = (bf16[1728,256]{1,0:T(8,128)(2,1)S(1)}, bf16[2816,128]{1,0:T(8,128)(2,1)S(1)}, bf16[2816,128]{1,0:T(8,128)(2,1)S(1)}) custom-call(bf16[1,2,8,64,128]{4,3,2,1,0:T(8,128)(2,1)S(1)} %get-tuple-element.21.pre_ref, bf16[1,1,4,32,128]{4,3,2,1,0:T(8,128)(2,1)S(1)} %get-tuple-element.22.og_ref, bf16[640,128]{1,0:T(8,128)(2,1)S(1)} %collective-permute-done.hx_ref, ...), custom_call_target="tpu_custom_call" | custom-call | flops 2000000000 | bytes 8000000 | tf_op jit(solution)/shard_map/main/pallas_call | solution.py:331
  17.2 2.5 %collective-permute-start.3 = (bf16[2816,128]{1,0:T(8,128)(2,1)S(1)}, bf16[2816,128]{1,0:T(8,128)(2,1)S(1)}, u32[]{:S(2)}, u32[]{:S(2)}) collective-permute-start(bf16[2816,128]{1,0:T(8,128)(2,1)S(1)} %get-tuple-element.29), channel_id=1, source_target_pairs={{0,64},{64,0},{1,65},{65,1},{2,66},{66,2},{3,67},{67,3},{4,68},{68... | collective-permute-start | bytes 2162696 | tf_op jit(solution)/shard_map/ppermute | solution.py:373
  19.7 2.0 %grad_input.1 = bf16[1,4,16,64,128]{4,3,2,1,0:T(8,128)(2,1)} custom-call(bf16[1728,256]{1,0:T(8,128)(2,1)S(1)} %get-tuple-element.30.a_ref, bf16[3,384,256]{2,1,0:T(8,128)(2,1)S(1)} %get-tuple-element.31.r1_ref), custom_call_target="tpu_custom_call" | custom-call | flops 1200000000 | bytes 3000000 | tf_op jit(solution)/shard_map/grad_input/pallas_call | solution.py:338
  21.7 0.0 collective-permute-done.3
  21.7 0.2 add_convert_fusion
  21.9 19.3 %all_to_all.15 = bf16[32,88,128]{2,1,0:T(8,128)(2,1)S(1)} all-to-all(bf16[32,88,128]{2,1,0:T(8,128)(2,1)S(1)} %bitcast.6), channel_id=1, replica_groups=mesh['xh'=2,'core'=2,'y'=4,'xl'=2,'zh'=4,'zl'=2] {'xh','y','xl','zl'}, dimensions={0} | all-to-all | bytes 1441792 | tf_op jit(solution)/shard_map/all_to_all | solution.py:379
  41.2 0.1 reduce_sum.24
  41.3 10.9 %all_to_all.16 = bf16[4,88,128]{2,1,0:T(8,128)(2,1)S(1)} all-to-all(bf16[4,88,128]{2,1,0:T(8,128)(2,1)S(1)} %broadcast_in_dim.4), channel_id=1, replica_groups=mesh['xh'=2,'core'=2,'y'=4,'xl'=2,'zh'=4,'zl'=2] {'zh'}, dimensions={0} | all-to-all | bytes 180224 | tf_op jit(solution)/shard_map/all_to_all | solution.py:381
  52.3 0.1 broadcast_in_dim.5
  52.4 15.1 %all_to_all.17 = bf16[32,88,128]{2,1,0:T(8,128)(2,1)S(1)} all-to-all(bf16[32,88,128]{2,1,0:T(8,128)(2,1)S(1)} %broadcast_in_dim.5), channel_id=1, replica_groups=mesh['xh'=2,'core'=2,'y'=4,'xl'=2,'zh'=4,'zl'=2] {'xh','y','xl','zl'}, dimensions={0} | all-to-all | bytes 1441792 | tf_op jit(solution)/shard_map/all_to_all | solution.py:383
  67.5 3.6 %collective-permute-start.4 = (bf16[2816,128]{1,0:T(8,128)(2,1)S(1)}, bf16[2816,128]{1,0:T(8,128)(2,1)S(1)}, u32[]{:S(2)}, u32[]{:S(2)}) collective-permute-start(bf16[2816,128]{1,0:T(8,128)(2,1)S(1)} %bitcast.4), channel_id=1, source_target_pairs={{0,64},{64,0},{1,65},{65,1},{2,66},{66,2},{3,67},{67,3},{4,68},{68... | collective-permute-start | bytes 2162696 | tf_op jit(solution)/shard_map/ppermute | solution.py:385
  71.1 1.1 %output.2 = (f32[1728,128]{1,0:T(8,128)}, f32[3456,128]{1,0:T(8,128)}) custom-call(bf16[2816,128]{1,0:T(8,128)(2,1)S(1)} %bitcast.5), custom_call_target="tpu_custom_call" | custom-call | bytes 2000000 | tf_op jit(solution)/shard_map/output/pallas_call | solution.py:343
  72.1 0.7 %collective-permute-done.4.half_ref = bf16[2816,128]{1,0:T(8,128)(2,1)S(1)} collective-permute-done((bf16[2816,128]{1,0:T(8,128)(2,1)S(1)}, bf16[2816,128]{1,0:T(8,128)(2,1)S(1)}, u32[]{:S(2)}, u32[]{:S(2)}) %collective-permute-start.4) | collective-permute-done | bytes 720928 | tf_op jit(solution)/shard_map/ppermute | solution.py:385
  72.9 1.1 %output.3 = (f32[1728,128]{1,0:T(8,128)}, f32[3456,128]{1,0:T(8,128)}) custom-call(bf16[2816,128]{1,0:T(8,128)(2,1)S(1)} %collective-permute-done.4.half_ref, f32[1728,128]{1,0:T(8,128)} %get-tuple-element.35.refs_0_, f32[3456,128]{1,0:T(8,128)} %get-tuple-element.36.refs_1_), custom_call_target="tpu_custom_call", output_to_operand_aliasing={{0}: (1, {}), {1}: (2, {})} | custom-call | bytes 2000000 | tf_op jit(solution)/shard_map/output/pallas_call | solution.py:343
  (2 shorter events, 0.0 us)
Async XLA Ops:
  1.7 13.7 %collective-permute-start = (bf16[640,128]{1,0:T(8,128)(2,1)S(1)}, bf16[640,128]{1,0:T(8,128)(2,1)S(1)}, u32[]{:S(2)}, u32[]{:S(2)}) collective-permute-start(bf16[640,128]{1,0:T(8,128)(2,1)S(1)} %get-tuple-element.23), channel_id=1, source_target_pairs={{8,0},{16,8},{24,16},{32,24},{40,32},{48,40},{56,48},{0,56},{9,1},... | collective-permute-start | bytes 491528 | tf_op jit(solution)/shard_map/ppermute | solution.py:368
  6.3 9.2 %collective-permute-start.1 = (bf16[160,128]{1,0:T(8,128)(2,1)S(1)}, bf16[160,128]{1,0:T(8,128)(2,1)S(1)}, u32[]{:S(2)}, u32[]{:S(2)}) collective-permute-start(bf16[160,128]{1,0:T(8,128)(2,1)S(1)} %get-tuple-element.24), channel_id=1, source_target_pairs={{1,0},{2,1},{3,2},{4,3},{5,4},{6,5},{7,6},{0,7},{9,8},{10,9},{11,1... | collective-permute-start | bytes 122888 | tf_op jit(solution)/shard_map/ppermute | solution.py:370
  11.8 3.6 %collective-permute-start.2 = (bf16[96,128]{1,0:T(8,128)(2,1)S(1)}, bf16[96,128]{1,0:T(8,128)(2,1)S(1)}, u32[]{:S(2)}, u32[]{:S(2)}) collective-permute-start(bf16[96,128]{1,0:T(8,128)(2,1)S(1)} %get-tuple-element.25), channel_id=1, source_target_pairs={{9,0},{10,1},{11,2},{12,3},{13,4},{14,5},{15,6},{8,7},{17,8},{18,9... | collective-permute-start | bytes 73736 | tf_op jit(solution)/shard_map/ppermute | solution.py:369
  17.2 4.5 %collective-permute-start.3 = (bf16[2816,128]{1,0:T(8,128)(2,1)S(1)}, bf16[2816,128]{1,0:T(8,128)(2,1)S(1)}, u32[]{:S(2)}, u32[]{:S(2)}) collective-permute-start(bf16[2816,128]{1,0:T(8,128)(2,1)S(1)} %get-tuple-element.29), channel_id=1, source_target_pairs={{0,64},{64,0},{1,65},{65,1},{2,66},{66,2},{3,67},{67,3},{4,68},{68... | collective-permute-start | bytes 2162696 | tf_op jit(solution)/shard_map/ppermute | solution.py:373
  67.5 5.4 %collective-permute-start.4 = (bf16[2816,128]{1,0:T(8,128)(2,1)S(1)}, bf16[2816,128]{1,0:T(8,128)(2,1)S(1)}, u32[]{:S(2)}, u32[]{:S(2)}) collective-permute-start(bf16[2816,128]{1,0:T(8,128)(2,1)S(1)} %bitcast.4), channel_id=1, source_target_pairs={{0,64},{64,0},{1,65},{65,1},{2,66},{66,2},{3,67},{67,3},{4,68},{68... | collective-permute-start | bytes 2162696 | tf_op jit(solution)/shard_map/ppermute | solution.py:385
